TPU v7x, 32 devices: a whole 2x2x4 slice. The times are simulated.
32 devices in a mesh: rows: 16 (over z, x, core), tm: 2 (over y).
Axes of the slice: x: 2, y: 2, z: 4, core: 2. Of those that a mesh axis runs over, the one named last changes fastest.
Arguments:
- patches: bfloat16 [16, 1024, 768], P('rows', 'tm'), may hold values from -6 to 6
- segment_ids: int32 [16, 1024], P('rows', 'tm'), may hold values from 0 to 5, never falling along the last dimension, each value on 1 to 512 neighbouring positions
- mask_positions: int32 [16, 409], P('rows'), may hold values from 0 to 1023, as said below
- mask_embed: bfloat16 [768], replicated, may hold values from -6 to 6
- norm1_gain: bfloat16 [768], replicated, may hold values from 0.5 to 1.5
- norm1_bias: bfloat16 [768], replicated, may hold values from -3 to 3
- w_qkv: bfloat16 [768, 2304], replicated, may hold values from -0.21875 to 0.21875
- query_bias: bfloat16 [768], replicated, may hold values from -3 to 3
- value_bias: bfloat16 [768], replicated, may hold values from -3 to 3
- w_out: bfloat16 [768, 768], replicated, may hold values from -1.75 to 1.75
- out_bias: bfloat16 [768], replicated, may hold values from -3 to 3
- norm2_gain: bfloat16 [768], replicated, may hold values from 0.5 to 1.5
- norm2_bias: bfloat16 [768], replicated, may hold values from -3 to 3
- w_up: bfloat16 [768, 3072], replicated, may hold values from -0.21875 to 0.21875
- up_bias: bfloat16 [3072], replicated, may hold values from -3 to 3
- w_down: bfloat16 [3072, 768], replicated, may hold values from -0.109375 to 0.109375
- down_bias: bfloat16 [768], replicated, may hold values from -3 to 3
- cotangent: bfloat16 [16, 1024, 768], P('rows', 'tm'), may hold values from -6 to 6
Outputs:
- output: bfloat16 [16, 1024, 768], P('rows', 'tm')
- grad_patches: bfloat16 [16, 1024, 768], P('rows', 'tm')
- grad_mask_embed: float32 [768], P('tm')
- grad_norm1_gain: float32 [768], P('tm')
- grad_norm1_bias: float32 [768], P('tm')
- grad_w_qkv: float32 [768, 2304], P('tm')
- grad_query_bias: float32 [768], P('tm')
- grad_value_bias: float32 [768], P('tm')
- grad_w_out: float32 [768, 768], P('tm')
- grad_out_bias: float32 [768], P('tm')
- grad_norm2_gain: float32 [768], P('tm')
- grad_norm2_bias: float32 [768], P('tm')
- grad_w_up: float32 [768, 3072], P('tm')
- grad_up_bias: float32 [3072], P('tm')
- grad_w_down: float32 [3072, 768], P('tm')
- grad_down_bias: float32 [768], P('tm')
Inputs may be any that keep to these rules, and one draw needn't show every extreme that they name: `mask_positions`: the 409 positions of a row are distinct. `segment_ids`: ids never fall along a row; every row has 6 segments.
All inputs are finite; a program needn't handle non-finite values.
Results may differ from a plain program's by a relative error of at most 0.019.
Values may be sent and summed in bfloat16 or wider, within the bound.
A program may use at most 128 MiB of HBM per device.

v0:
```python
from functools import partial
import math

import jax
import jax.numpy as jnp
from jax import lax
from jax.experimental import pallas as pl
from jax.experimental.pallas import tpu as pltpu
from jax.sharding import PartitionSpec as P

HEADS = 12
HEAD = 64


norm_eps = 1e-06
neg_large = -1e30


def normalize(values):
    center = values - jnp.mean(values, axis=-1, keepdims=True)
    scale_inv = lax.rsqrt(jnp.mean(center * center, axis=-1, keepdims=True) + norm_eps)
    return (center * scale_inv, scale_inv)


def norm_back(grad_out, normed, scale_inv, norm_gain):
    grad_normed = grad_out * norm_gain
    mean_one = jnp.mean(grad_normed, axis=-1, keepdims=True)
    mean_two = jnp.mean(grad_normed * normed, axis=-1, keepdims=True)
    return scale_inv * (grad_normed - mean_one - normed * mean_two)


def split_heads(tensor):
    rows_n, length, width = tensor.shape
    return tensor.reshape(rows_n, length, HEADS, width // HEADS).transpose(2, 0, 1, 3)


def join_heads(tensor):
    heads_n, rows_n, length, size = tensor.shape
    return tensor.transpose(1, 2, 0, 3).reshape(rows_n, length, heads_n * size)


def head_scores(query, keys_h, same):
    scores = jnp.einsum("rqd,rkd->rqk", query, keys_h, preferred_element_type=jnp.float32)
    return jnp.where(same, scores, neg_large)


def attend_forward(query_heads, key_heads, value_heads, same):

    def one_head(operands):
        query, keys_h, values_h = operands
        scores = head_scores(query, keys_h, same)
        peak = jnp.max(scores, axis=-1, keepdims=True)
        total = jnp.sum(jnp.exp(scores - peak), axis=-1, keepdims=True)
        log_total = peak + jnp.log(total)
        weights = jnp.exp(scores - log_total).astype(jnp.bfloat16)
        result = jnp.einsum("rqk,rkd->rqd", weights, values_h, preferred_element_type=jnp.float32)
        return (result, log_total[..., 0])

    return lax.map(one_head, (query_heads, key_heads, value_heads))


def attend_backward(query_heads, key_heads, value_heads, grad_heads, log_totals, same):

    def one_head(operands):
        query, keys_h, values_h, grad_out, log_total = operands
        scores = head_scores(query, keys_h, same)
        probs_full = jnp.exp(scores - log_total[..., None])
        probs_low = probs_full.astype(jnp.bfloat16)
        grad_values = jnp.einsum(
            "rqk,rqd->rkd", probs_low, grad_out, preferred_element_type=jnp.float32
        )
        grad_probs = jnp.einsum(
            "rqd,rkd->rqk", grad_out, values_h, preferred_element_type=jnp.float32
        )
        delta = jnp.sum(grad_probs * probs_full, axis=-1, keepdims=True)
        grad_scores = (probs_full * (grad_probs - delta)).astype(jnp.bfloat16)
        grad_query = jnp.einsum(
            "rqk,rkd->rqd", grad_scores, keys_h, preferred_element_type=jnp.float32
        )
        grad_keys = jnp.einsum(
            "rqk,rqd->rkd", grad_scores, query, preferred_element_type=jnp.float32
        )
        return (grad_query, grad_keys, grad_values)

    return lax.map(one_head, (query_heads, key_heads, value_heads, grad_heads, log_totals))


MESH = pl.DeviceIdType.MESH
SUB = 96
COLS = 384
LAGS = (0, 1, 3, 4, 5, 7, 8, 9)


def places():
    row = lax.axis_index("rows")
    y = lax.axis_index("tm")
    core = row % 2
    x = (row // 2) % 2
    z_low = (row // 4) % 2
    z_high = row // 8
    peers = (
        (row + 1 - 2 * core, y),
        (row, 1 - y),
        (row + 2 - 4 * x, y),
        (row + 4 - 8 * z_low, y),
        (row + 8 - 16 * z_high, y),
    )
    return core, x, y, peers


def greet(peers):
    barrier = pltpu.get_barrier_semaphore()
    for peer in peers:
        pl.semaphore_signal(barrier, inc=1, device_id=peer, device_id_type=MESH)
    pl.semaphore_wait(barrier, len(peers))


def total_rows(tensor):
    return jnp.sum(tensor.astype(jnp.float32), axis=(0, 1))


VMEM = pltpu.VMEM
F32 = jnp.float32
BF16 = jnp.bfloat16
HALF = 512
TILE = 256
R_EMBED, R_G1, R_B1, R_QB, R_VB, R_OB, R_G2, R_B2, R_DB, R_UB = 0, 1, 2, 3, 4, 5, 6, 7, 8, 9
QUERY_SCALE = 1.0 / math.sqrt(HEAD)


def dot(a, b):
    return lax.dot_general(a, b, (((1,), (0,)), ((), ())), preferred_element_type=F32)


def dot_t(a, b):
    return lax.dot_general(a, b, (((1,), (1,)), ((), ())), preferred_element_type=F32)


def t_dot(a, b):
    return lax.dot_general(a, b, (((0,), (0,)), ((), ())), preferred_element_type=F32)


def standard(values):
    center = values - jnp.mean(values, axis=-1, keepdims=True)
    scale_inv = lax.rsqrt(jnp.mean(center * center, axis=-1, keepdims=True) + norm_eps)
    return center * scale_inv, scale_inv


def masked_inputs(patch, first, marks, embed):
    at = first + lax.broadcasted_iota(jnp.int32, (patch.shape[0], 1), 0)
    flagged = jnp.max(jnp.where(at == marks, 1.0, 0.0), axis=-1, keepdims=True) > 0.5
    return flagged, jnp.where(flagged, embed, patch.astype(F32))


def front_kernel(other, p_ref, marks_ref, table_ref, w_ref, h1_ref, qkv_ref):
    y = lax.axis_index("tm")
    first = (1 - y if other else y) * HALF + pl.program_id(0) * TILE
    unused, inputs = masked_inputs(p_ref[...], first, marks_ref[...], table_ref[R_EMBED : R_EMBED + 1, :])
    normed, unused = standard(inputs)
    hidden = (normed * table_ref[R_G1 : R_G1 + 1, :] + table_ref[R_B1 : R_B1 + 1, :]).astype(BF16)
    h1_ref[...] = hidden
    for part in range(6):
        cols = slice(part * 384, part * 384 + 384)
        project = dot(hidden, w_ref[:, cols])
        bias = slice((part % 2) * 384, (part % 2) * 384 + 384)
        if part < 2:
            project = (project + table_ref[R_QB : R_QB + 1, bias]) * QUERY_SCALE
        elif part >= 4:
            project = project + table_ref[R_VB : R_VB + 1, bias]
        qkv_ref[:, cols] = project.astype(BF16)


def front(other, patch, marks, table, w_qkv):
    return pl.pallas_call(
        partial(front_kernel, other),
        grid=(HALF // TILE,),
        out_shape=(
            jax.ShapeDtypeStruct((HALF, 768), BF16),
            jax.ShapeDtypeStruct((HALF, 2304), BF16),
        ),
        in_specs=[
            pl.BlockSpec((TILE, 768), lambda i: (i, 0)),
            pl.BlockSpec(marks.shape, lambda i: (0, 0)),
            pl.BlockSpec(table.shape, lambda i: (0, 0)),
            pl.BlockSpec((768, 2304), lambda i: (0, 0), pipeline_mode=pl.Buffered(1)),
        ],
        out_specs=(
            pl.BlockSpec((TILE, 768), lambda i: (i, 0)),
            pl.BlockSpec((TILE, 2304), lambda i: (i, 0)),
        ),
        cost_estimate=pl.CostEstimate(flops=2 * HALF * 768 * 2304, bytes_accessed=8 << 20, transcendentals=0),
    )(patch, marks, table, w_qkv)


def attend_kernel(q_ref, k_ref, v_ref, kx_ref, vx_ref, qa_ref, ka_ref, kxa_ref, o_ref, lse_ref):
    y = lax.axis_index("tm")
    pair = pl.program_id(0)
    lane = lax.broadcasted_iota(jnp.int32, (1, 128), 1)
    keys = jnp.concatenate([k_ref[...], ka_ref[...]], axis=1)
    far_keys = jnp.concatenate([kx_ref[...], kxa_ref[...]], axis=1)
    near_x = pl.multiple_of(y * TILE, TILE)
    near_keys = jnp.concatenate([kx_ref[pl.ds(near_x, TILE), :], kxa_ref[pl.ds(near_x, TILE), :]], axis=1)
    for far in range(2):
        rows = pl.ds(pl.multiple_of((y if far else 1 - y) * TILE, TILE), TILE)
        q = q_ref[rows, :]
        qa = qa_ref[rows, :]
        kept = None
        marks = jnp.where(pair == 0, 0.0, lse_ref[rows, :])
        for h in range(2):
            mine = (lane // 64) == h
            query = jnp.concatenate([jnp.where(mine, q, 0), qa], axis=1)
            own = dot_t(query, keys)
            cross = dot_t(query, near_keys if far else far_keys)
            peak = jnp.maximum(jnp.max(own, axis=-1, keepdims=True), jnp.max(cross, axis=-1, keepdims=True))
            own = jnp.exp(own - peak)
            cross = jnp.exp(cross - peak)
            total = jnp.sum(own, axis=-1, keepdims=True) + jnp.sum(cross, axis=-1, keepdims=True)
            values = vx_ref[pl.ds(near_x, TILE), :] if far else vx_ref[...]
            out = dot(own.astype(BF16), v_ref[...]) + dot(cross.astype(BF16), values)
            out = out / total
            kept = out if h == 0 else jnp.where(mine, out, kept)
            marks = jnp.where(lane == 2 * pair + h, peak + jnp.log(total), marks)
        o_ref[rows, :] = kept.astype(BF16)
        lse_ref[rows, :] = marks


def attend(qkv, qkv_other, qa, ka, kxa):
    def block(first):
        return pl.BlockSpec((HALF, 128), lambda i: (0, first + i))

    whole = pl.BlockSpec((HALF, 128), lambda i: (0, 0))
    return pl.pallas_call(
        attend_kernel,
        grid=(6,),
        out_shape=(jax.ShapeDtypeStruct((HALF, 768), BF16), jax.ShapeDtypeStruct((HALF, 128), F32)),
        in_specs=[block(0), block(6), block(12), block(6), block(12), whole, whole, whole],
        out_specs=(pl.BlockSpec((HALF, 128), lambda i: (0, i)), whole),
        cost_estimate=pl.CostEstimate(
            flops=4 * 12 * HALF * 1024 * 64, bytes_accessed=8 << 20, transcendentals=12 * HALF * 1024
        ),
    )(qkv, qkv, qkv, qkv_other, qkv_other, qa, ka, kxa)


ERFC_P = 0.3275911
ERFC_C = (
    0.1851102167482524,
    0.17993860771517878,
    0.21041948320823337,
    0.011498087426314028,
    0.47813345988158296,
    -0.4317659362057169,
    0.5111742647535956,
    -0.14450823957827402,
)


def gelu_and_slope(u):
    t = 1.0 / (1.0 + (ERFC_P * math.sqrt(0.5)) * jnp.abs(u))
    bell = jnp.exp(-0.5 * (u * u))
    series = ERFC_C[7]
    for c in ERFC_C[6::-1]:
        series = series * t + c
    tail = (0.5 * t) * series * bell
    phi = jnp.where(u < 0, tail, 1.0 - tail)
    return u * phi, phi + u * (bell * (1.0 / math.sqrt(2.0 * math.pi)))


FF_TILE = 384


def middle_kernel(
    p_ref, marks_ref, table_ref, a_ref, wo_ref, cot_ref, wu_ref, wd_ref, ub_ref, mid_ref, h2_ref, act_ref, gu_ref, ubs_ref
):
    y = lax.axis_index("tm")

    @pl.when(pl.program_id(0) == 0)
    def _():
        for tile in range(HALF // TILE):
            rows = slice(tile * TILE, tile * TILE + TILE)
            unused, inputs = masked_inputs(
                p_ref[rows, :], y * HALF + tile * TILE, marks_ref[...], table_ref[R_EMBED : R_EMBED + 1, :]
            )
            mid = inputs + dot(a_ref[rows, :], wo_ref[...]) + table_ref[R_OB : R_OB + 1, :]
            normed, unused = standard(mid)
            mid_ref[rows, :] = mid
            h2_ref[rows, :] = (normed * table_ref[R_G2 : R_G2 + 1, :] + table_ref[R_B2 : R_B2 + 1, :]).astype(BF16)

    sums = jnp.zeros((1, FF_TILE), F32)
    for tile in range(HALF // TILE):
        rows = slice(tile * TILE, tile * TILE + TILE)
        upper = dot(h2_ref[rows, :], wu_ref[...]) + ub_ref[...]
        value, slope = gelu_and_slope(upper)
        act_ref[rows, :] = value.astype(BF16)
        grad = dot_t(cot_ref[rows, :], wd_ref[...])
        low = (grad * slope).astype(BF16)
        gu_ref[rows, :] = low
        sums = sums + jnp.sum(low.astype(F32), axis=0, keepdims=True)
    ubs_ref[...] = sums


def middle_part(patch, marks, table, attended, w_out, cot, w_up, w_down, up_bias):
    def full(shape):
        return pl.BlockSpec(shape, lambda i: (0, 0))

    return pl.pallas_call(
        middle_kernel,
        grid=(3072 // FF_TILE,),
        out_shape=(
            jax.ShapeDtypeStruct((HALF, 768), F32),
            jax.ShapeDtypeStruct((HALF, 768), BF16),
            jax.ShapeDtypeStruct((HALF, 3072), BF16),
            jax.ShapeDtypeStruct((HALF, 3072), BF16),
            jax.ShapeDtypeStruct((1, 3072), F32),
        ),
        in_specs=[
            full((HALF, 768)),
            full(marks.shape),
            full(table.shape),
            full((HALF, 768)),
            full((768, 768)),
            full((HALF, 768)),
            pl.BlockSpec((768, FF_TILE), lambda i: (0, i)),
            pl.BlockSpec((FF_TILE, 768), lambda i: (i, 0)),
            pl.BlockSpec((1, FF_TILE), lambda i: (0, i)),
        ],
        out_specs=(
            full((HALF, 768)),
            full((HALF, 768)),
            pl.BlockSpec((HALF, FF_TILE), lambda i: (0, i)),
            pl.BlockSpec((HALF, FF_TILE), lambda i: (0, i)),
            pl.BlockSpec((1, FF_TILE), lambda i: (0, i)),
        ),
        cost_estimate=pl.CostEstimate(
            flops=2 * HALF * 768 * (768 + 6144), bytes_accessed=24 << 20, transcendentals=HALF * 3072
        ),
    )(patch, marks, table, attended, w_out, cot, w_up, w_down, up_bias)


CHUNKS = 24
T_OWN = 6
T_LAST = 24
T_VEC = 28


def halves_kernel(
    act_h, cot_h, gu_h, mid_h, h2_h, wo_h, qkv_h, qkvx_h, att_h, h1_h, patch_h, wq_h, wu_h, wd_h,
    qa_ref, ka_ref, qxa_ref, kxa_ref, lse_ref, lsex_ref, table_ref, marks_ref, ub_ref,
    parts_h, out_h, gp_h, vec_out,
    act, cot, gu, mid, h2, wo, qkv, qkvx, att, h1, patch, wq, wu, wd,
    acc, gb, do, dox, dqkv, dq, dk, dv, drow, dxrow,
    g, r1, r2, r3, r4, r5, done, v0, v1, v2,
    insem, wusem, wdsem, ssem, rsem, vs, vr, xs, xr, outsem, lastsem,
):
    core, x, y, peers = places()
    pair, yp, xp, zp1, zp2 = peers
    lane = lax.broadcasted_iota(jnp.int32, (1, 128), 1)
    inputs = (
        (act_h, act), (cot_h, cot), (gu_h, gu), (mid_h, mid), (h2_h, h2), (wo_h, wo),
        (qkv_h, qkv), (att_h, att), (qkvx_h, qkvx), (h1_h, h1), (patch_h, patch), (wq_h, wq),
    )
    ACT, COT, GU, MID, H2, WO, QKV, ATT, QKVX, H1, PATCH, WQ = range(12)

    def load(i):
        return pltpu.make_async_copy(inputs[i][0], inputs[i][1], insem.at[i])

    def up_tile(k):
        cols = pl.ds(pl.multiple_of(k * 512, 512), 512)
        return pltpu.make_async_copy(wu_h.at[:, cols], wu.at[k % 2], wusem.at[k % 2])

    def down_tile(k):
        rows = pl.ds(pl.multiple_of(k * 512, 512), 512)
        return pltpu.make_async_copy(wd_h.at[rows, :], wd.at[k % 2], wdsem.at[k % 2])

    for i in (ACT, COT, GU):
        load(i).start()
    up_tile(0).start()
    up_tile(1).start()
    for i in (MID, H2, WO, QKV, ATT, QKVX, H1, PATCH, WQ):
        load(i).start()
    down_tile(0).start()
    down_tile(1).start()
    greet(peers)

    def remote(src, dst, send, recv, dev):
        return pltpu.make_async_remote_copy(
            src_ref=src, dst_ref=dst, send_sem=send, recv_sem=recv, device_id=dev, device_id_type=MESH
        )

    def copy(s, c):
        src, dst, dev = (
            lambda: (g.at[c % 4, 1 - core], r1.at[c], pair),
            lambda: (r1.at[c, 1 - y], r2.at[c], yp),
            lambda: (r2.at[c, 1 - x], r3.at[c], xp),
            lambda: (r3.at[c], r4.at[c], zp1),
            lambda: (r4.at[c], r5.at[c], zp2),
            lambda: (done.at[c, core, x], done.at[c, core, x], xp),
            lambda: (done.at[c, core], done.at[c, core], pair),
        )[s]()
        return remote(src, dst, ssem.at[s, c], rsem.at[s, c], dev)

    def part_out(c):
        return pltpu.make_async_copy(done.at[c], parts_h.at[c], outsem.at[c])

    def stage(s, c):
        if s > 0:
            copy(s - 1, c).wait_recv()
        if s == 1:
            r1[c] = r1[c] + g[c % 4, core]
        elif s == 2:
            r2[c] = r2[c] + r1[c, y]
        elif s == 3:
            r3[c] = r3[c] + r2[c, x]
        elif s == 4:
            r4[c] = r4[c] + r3[c]
        elif s == 5:
            done[c, core, x] = r5[c] + r4[c]
        elif s == 7:
            copy(5, c).wait_send()
            copy(6, c).wait_send()
            part_out(c).start()
        if s < 7:
            copy(s, c).start()

    def vec_copy(s):
        src, dst, dev = (
            lambda: (v0, v1, pair),
            lambda: (v1.at[1 - y], v2.at[0], yp),
            lambda: (v2.at[0], v2.at[1], xp),
            lambda: (v2.at[1], v2.at[2], zp1),
            lambda: (v2.at[2], v2.at[3], zp2),
        )[s]()
        return remote(src, dst, vs.at[s], vr.at[s], dev)

    def vec_stage(s):
        if s > 0:
            vec_copy(s - 1).wait_recv()
        if s == 1:
            v1[...] = v1[...] + v0[...]
        elif s == 2:
            v2[0] = v2[0] + v1[y]
        elif s == 5:
            vec_out[...] = v2[3] + v2[2]
        elif s > 2:
            v2[s - 2] = v2[s - 2] + v2[s - 3]
        if s < 5:
            vec_copy(s).start()

    def far_copy(i):
        src, dst = ((do, dox), (drow, dxrow))[i]
        return remote(src, dst, xs.at[i], xr.at[i], yp)

    def row(r):
        return table_ref[r : r + 1, :]

    def add_vec(r, value):
        for half in range(2):
            v0[half, r : r + 1, :] = v0[half, r : r + 1, :] + value[:, half * 384 : half * 384 + 384]

    def emit(left, right, c):
        number = right.shape[1] // 384
        for i in range(number):

            @pl.when(c + i >= 4)
            def _():
                copy(0, c + i - 4).wait_send()

        for half in range(2):
            block = t_dot(left(half), right).astype(BF16)
            for i in range(number):
                for other in range(4):
                    rows = slice(other * SUB, other * SUB + SUB)
                    g[(c + i) % 4, other // 2, half, other % 2] = block[rows, i * 384 : i * 384 + 384]

    def lanes(start, size=128):
        return pl.ds(pl.multiple_of(start, 128), size)

    def grad_hidden(k):
        up_tile(k).wait()
        for tile in range(2):
            rows = slice(tile * 256, tile * 256 + 256)
            acc[rows, :] = acc[rows, :] + dot_t(gu[rows, lanes(k * 512, 512)], wu[k % 2])

        @pl.when(k + 2 < 6)
        def _():
            up_tile(k + 2).start()

    def second_norm():
        def tile(i, carry):
            rows = pl.ds(pl.multiple_of(i * 128, 128), 128)
            normed, inverse = standard(mid[rows, :])
            grad = acc[rows, :]
            cotangent = cot[rows, :].astype(F32)
            add_vec(6, jnp.sum(grad * normed, axis=0, keepdims=True))
            add_vec(7, jnp.sum(grad, axis=0, keepdims=True))
            add_vec(8, jnp.sum(cotangent, axis=0, keepdims=True))
            total = cotangent + norm_back(grad, normed, inverse, row(R_G2))
            acc[rows, :] = total
            low = total.astype(BF16)
            gb[rows, :] = low
            add_vec(5, jnp.sum(low.astype(F32), axis=0, keepdims=True))
            return carry

        lax.fori_loop(0, 4, tile, 0)

    def grad_attended():
        for tile in range(2):
            rows = slice(tile * 256, tile * 256 + 256)
            do[rows, :] = dot_t(gb[rows, :], wo[...]).astype(BF16)
        for tile in range(4):
            rows = slice(tile * 128, tile * 128 + 128)
            columns = jnp.zeros((128, 128), F32)
            for p in range(6):
                cols = slice(p * 128, p * 128 + 128)
                product = do[rows, cols].astype(F32) * att[rows, cols].astype(F32)
                for h in range(2):
                    total = jnp.sum(jnp.where((lane // 64) == h, product, 0.0), axis=1, keepdims=True)
                    columns = jnp.where(lane == 2 * p + h, total, columns)
            drow[:, rows] = columns.T[:16, :]
        far_copy(0).start()
        far_copy(1).start()

    def piece(keys, key_mask, values, query, query_mask, grad, lse, delta):
        scores = dot_t(jnp.concatenate([keys, key_mask], axis=1), jnp.concatenate([query, query_mask], axis=1))
        probs = jnp.exp(scores - lse)
        grad_scores = probs * (dot_t(values, grad) - delta)
        return probs.astype(BF16), grad_scores.astype(BF16)

    def own_pair(p):
        slot = p % 3

        def head(h, carry):
            mine = (lane // 64) == h
            stat = pl.ds(2 * p + h, 1)
            query = jnp.where(mine, qkv[:, lanes(p * 128)], 0)
            grad = jnp.where(mine, do[:, lanes(p * 128)], 0)
            for tile in range(2):
                rows = slice(tile * 256, tile * 256 + 256)
                keys = qkv[rows, lanes(768 + p * 128)]
                probs, scores = piece(
                    keys, ka_ref[rows, :], qkv[rows, lanes(1536 + p * 128)], query, qa_ref[...], grad,
                    lse_ref[stat, :], drow[stat, :],
                )
                new = dot(scores, query)
                dk[slot, rows, :] = jnp.where(h == 0, new, dk[slot, rows, :] + new)
                new = dot(probs, grad)
                dv[slot, rows, :] = jnp.where(h == 0, new, dv[slot, rows, :] + new)
                new = t_dot(scores, jnp.where(mine, keys, 0))
                dq[slot] = jnp.where((h == 0) & (tile == 0), new, dq[slot] + new)
            return carry

        lax.fori_loop(0, 2, head, 0)

    def far_pair(p):
        slot = p % 3
        near, far = pl.multiple_of((1 - y) * 256, 256), pl.multiple_of(y * 256, 256)

        def head(h, carry):
            mine = (lane // 64) == h
            stat = pl.ds(2 * p + h, 1)
            for first, start, size in ((far, 0, 512), (near, near, 256)):
                rows, others = pl.ds(first, 256), pl.ds(start, size)
                query = jnp.where(mine, qkv[others, lanes(p * 128)], 0)
                grad = jnp.where(mine, do[others, lanes(p * 128)], 0)
                keys = qkvx[rows, lanes(768 + p * 128)]
                probs, scores = piece(
                    keys, kxa_ref[rows, :], qkvx[rows, lanes(1536 + p * 128)], query, qa_ref[others, :], grad,
                    lse_ref[stat, others], drow[stat, others],
                )
                dq[slot, others, :] = dq[slot, others, :] + t_dot(scores, jnp.where(mine, keys, 0))
            for first, start, size in ((near, 0, 512), (far, far, 256)):
                rows, others = pl.ds(first, 256), pl.ds(start, size)
                query = jnp.where(mine, qkvx[others, lanes(p * 128)], 0)
                grad = jnp.where(mine, dox[others, lanes(p * 128)], 0)
                probs, scores = piece(
                    qkv[rows, lanes(768 + p * 128)], ka_ref[rows, :], qkv[rows, lanes(1536 + p * 128)],
                    query, qxa_ref[others, :], grad, lsex_ref[stat, others], dxrow[stat, others],
                )
                dk[slot, rows, :] = dk[slot, rows, :] + dot(scores, query)
                dv[slot, rows, :] = dv[slot, rows, :] + dot(probs, grad)
            return carry

        lax.fori_loop(0, 2, head, 0)
        dqkv[:, lanes(p * 128)] = (dq[slot].astype(BF16).astype(F32) * QUERY_SCALE).astype(BF16)
        dqkv[:, lanes(768 + p * 128)] = dk[slot].astype(BF16)
        dqkv[:, lanes(1536 + p * 128)] = dv[slot].astype(BF16)

    def output_tile(k):
        down_tile(k).wait()
        for tile in range(2):
            rows = slice(tile * 256, tile * 256 + 256)
            mid[rows, :] = mid[rows, :] + dot(act[rows, lanes(k * 512, 512)], wd[k % 2])

        @pl.when(k + 2 < 6)
        def _():
            down_tile(k + 2).start()

    def store_output():
        for tile in range(4):
            rows = slice(tile * 128, tile * 128 + 128)
            gb[rows, :] = (mid[rows, :] + row(R_DB)).astype(BF16)
        pltpu.make_async_copy(gb, out_h, lastsem.at[0]).start()

    def grad_first(part):
        for tile in range(2):
            rows = slice(tile * 256, tile * 256 + 256)
            new = dot_t(dqkv[rows, lanes(part * 768, 768)], wq[:, lanes(part * 768, 768)])
            mid[rows, :] = jnp.where(part == 0, new, mid[rows, :] + new)

    def first_norm():
        def tile(i, carry):
            rows = pl.ds(pl.multiple_of(i * 128, 128), 128)
            flagged, values = masked_inputs(patch[rows, :], y * HALF + i * 128, marks_ref[...], row(R_EMBED))
            normed, inverse = standard(values)
            grad = mid[rows, :]
            add_vec(1, jnp.sum(grad * normed, axis=0, keepdims=True))
            add_vec(2, jnp.sum(grad, axis=0, keepdims=True))
            total = acc[rows, :] + norm_back(grad, normed, inverse, row(R_G1))
            add_vec(0, jnp.sum(jnp.where(flagged, total, 0.0), axis=0, keepdims=True))
            att[rows, :] = jnp.where(flagged, 0.0, total).astype(BF16)
            add_vec(3, jnp.sum(dqkv[rows, :768].astype(F32), axis=0, keepdims=True))
            add_vec(4, jnp.sum(dqkv[rows, 1536:].astype(F32), axis=0, keepdims=True))
            return carry

        lax.fori_loop(0, 4, tile, 0)
        pltpu.make_async_copy(att, gp_h, lastsem.at[1]).start()

    acc[...] = jnp.zeros_like(acc)
    v0[...] = jnp.zeros_like(v0)
    for half in range(2):
        for i in range(4):
            start = half * 1536 + i * 384
            v0[half, 9 + i : 10 + i, :] = ub_ref[:, start : start + 384]
    load(ACT).wait()
    load(COT).wait()

    def step(t, carry):
        even = t % 2 == 0

        @pl.when((t < 8) & even)
        def _():
            start = t * 192
            emit(lambda half: act[:, lanes(half * 1536 + start, 384)], cot[...], t)

        @pl.when((t >= 8) & (t < 16) & even)
        def _():
            emit(lambda half: h2[:, half * 384 : half * 384 + 384], gu[:, lanes((t - 8) * 384, 768)], t)

        @pl.when(t == 16)
        def _():
            emit(lambda half: att[:, half * 384 : half * 384 + 384], gb[...], t)

        @pl.when((t >= 18) & (t < 24))
        def _():
            p = t - 18
            right = jnp.concatenate([dqkv[:, lanes(part * 768 + p * 128)] for part in range(3)], axis=1)
            emit(lambda half: h1[:, half * 384 : half * 384 + 384], right, t)

        for s in range(2):
            c = t - LAGS[s]

            @pl.when((c >= 0) & (c < CHUNKS))
            def _():
                stage(s, c)

        @pl.when(t == 0)
        def _():
            load(GU).wait()

        @pl.when(t < 3)
        def _():
            grad_hidden(2 * t)
            grad_hidden(2 * t + 1)

        @pl.when(t == 3)
        def _():
            load(MID).wait()
            second_norm()

        @pl.when(t == 4)
        def _():
            for i in (WO, ATT):
                load(i).wait()
            grad_attended()

        u = t - T_OWN

        @pl.when(u == 0)
        def _():
            for i in (H2, QKV, QKVX, H1, PATCH, WQ):
                load(i).wait()

        @pl.when((u >= 0) & ((u <= 2) | ((u <= 8) & (u % 2 == 0))))
        def _():
            own_pair(jnp.where(u <= 2, u, (u + 2) // 2))

        @pl.when(u == 3)
        def _():
            far_copy(0).wait_recv()
            far_copy(1).wait_recv()

        @pl.when((u >= 3) & (u <= 11) & ((u >= 10) | (u % 2 == 1)))
        def _():
            far_pair(jnp.where(u <= 9, (u - 3) // 2, u - 6))

        @pl.when((t >= 18) & (t < 24))
        def _():
            output_tile(t - 18)

        @pl.when(t == 23)
        def _():
            store_output()

        @pl.when((t >= T_LAST) & (t < T_LAST + 3))
        def _():
            grad_first(t - T_LAST)

        @pl.when(t == T_LAST + 3)
        def _():
            first_norm()

        for s in range(2, 8):
            c = t - LAGS[s]

            @pl.when((c >= 0) & (c < CHUNKS))
            def _():
                stage(s, c)

        for s in range(6):

            @pl.when(t == T_VEC + s)
            def _():
                vec_stage(s)

        return carry

    lax.fori_loop(0, T_VEC + 6, step, 0)

    def drain(c, carry):
        for s in range(1, 5):
            copy(s, c).wait_send()
        part_out(c).wait()
        return carry

    lax.fori_loop(0, CHUNKS, drain, 0)
    for c in range(CHUNKS - 4, CHUNKS):
        copy(0, c).wait_send()
    for s in range(5):
        vec_copy(s).wait_send()
    for i in range(2):
        far_copy(i).wait_send()
    pltpu.make_async_copy(gb, out_h, lastsem.at[0]).wait()
    pltpu.make_async_copy(att, gp_h, lastsem.at[1]).wait()


def backward(big, weights, small):
    hbm = pl.BlockSpec(memory_space=pl.ANY)
    near = pl.BlockSpec(memory_space=pltpu.VMEM)

    def low(*shape):
        return pltpu.VMEM(shape, BF16)

    def full(*shape):
        return pltpu.VMEM(shape, F32)

    dma = pltpu.SemaphoreType.DMA
    held = [pltpu.VMEM(a.shape, a.dtype) for a in big]
    return pl.pallas_call(
        halves_kernel,
        out_shape=(
            jax.ShapeDtypeStruct((CHUNKS, 2, 2, SUB, COLS), BF16),
            jax.ShapeDtypeStruct((HALF, 768), BF16),
            jax.ShapeDtypeStruct((HALF, 768), BF16),
            jax.ShapeDtypeStruct((16, COLS), F32),
        ),
        in_specs=[hbm] * (len(big) + 2) + [near] * len(small),
        out_specs=(hbm, hbm, hbm, near),
        scratch_shapes=held
        + [
            low(2, 768, 512),
            low(2, 512, 768),
            full(HALF, 768),
            low(HALF, 768),
            low(HALF, 768),
            low(HALF, 768),
            low(HALF, 2304),
            full(3, HALF, 128),
            full(3, HALF, 128),
            full(3, HALF, 128),
            full(16, HALF),
            full(16, HALF),
            low(4, 2, 2, 2, SUB, COLS),
            low(CHUNKS, 2, 2, SUB, COLS),
            low(CHUNKS, 2, SUB, COLS),
            low(CHUNKS, SUB, COLS),
            low(CHUNKS, SUB, COLS),
            low(CHUNKS, SUB, COLS),
            low(CHUNKS, 2, 2, SUB, COLS),
            full(2, 16, COLS),
            full(2, 16, COLS),
            full(4, 16, COLS),
            dma((12,)),
            dma((2,)),
            dma((2,)),
            dma((7, CHUNKS)),
            dma((7, CHUNKS)),
            dma((5,)),
            dma((5,)),
            dma((2,)),
            dma((2,)),
            dma((CHUNKS,)),
            dma((2,)),
        ],
        compiler_params=pltpu.CompilerParams(
            collective_id=0, has_side_effects=True, vmem_limit_bytes=67043328
        ),
    )(*big, *weights, *small)


def widen_kernel(pair_ref, qkv_ref, down_ref, up_ref, out_ref, proj_ref):
    i = pl.program_id(0)
    for first, last, ref in ((0, 4, down_ref), (4, 8, up_ref), (8, 9, out_ref)):

        @pl.when((i >= first) & (i < last))
        def _():
            for c in range(2):
                ref[:, c * 384 : c * 384 + 384] = pair_ref[c].astype(F32)

    @pl.when(i >= 9)
    def _():
        for p in range(6):
            proj_ref[:, p * 128 : p * 128 + 128] = qkv_ref[p].astype(F32)


def widen(parts):
    parts = parts.reshape(CHUNKS, 384, COLS)
    return pl.pallas_call(
        widen_kernel,
        grid=(12,),
        out_shape=(
            jax.ShapeDtypeStruct((1536, 768), F32),
            jax.ShapeDtypeStruct((384, 3072), F32),
            jax.ShapeDtypeStruct((384, 768), F32),
            jax.ShapeDtypeStruct((384, 2304), F32),
        ),
        in_specs=[
            pl.BlockSpec((2, 384, COLS), lambda i: (jnp.minimum(i, 8), 0, 0)),
            pl.BlockSpec((6, 384, 128), lambda i: (3, 0, jnp.maximum(i - 9, 0))),
        ],
        out_specs=(
            pl.BlockSpec((384, 768), lambda i: (jnp.minimum(i, 3), 0)),
            pl.BlockSpec((384, 768), lambda i: (0, jnp.clip(i - 4, 0, 3))),
            pl.BlockSpec((384, 768), lambda i: (0, 0)),
            pl.BlockSpec((384, 768), lambda i: (0, jnp.maximum(i - 9, 0))),
        ),
    )(parts, parts)


def block_shards(
    patches,
    segment_ids,
    mask_positions,
    mask_embed,
    norm1_gain,
    norm1_bias,
    w_qkv,
    query_bias,
    value_bias,
    w_out,
    out_bias,
    norm2_gain,
    norm2_bias,
    w_up,
    up_bias,
    w_down,
    down_bias,
    cotangent,
):
    swap = [(0, 1), (1, 0)]
    width = 768
    patch = patches[0]
    cot = cotangent[0]
    patch_x = lax.ppermute(patch, "tm", swap)
    ids = segment_ids[0]
    ids_x = lax.ppermute(ids, "tm", swap)
    table = jnp.concatenate(
        [
            jnp.stack(
                [
                    mask_embed,
                    norm1_gain,
                    norm1_bias,
                    query_bias,
                    value_bias,
                    out_bias,
                    norm2_gain,
                    norm2_bias,
                    down_bias,
                ]
            ),
            up_bias.reshape(4, 768),
            jnp.zeros((3, 768), BF16),
        ]
    ).astype(F32)
    lane = jnp.arange(128)[None, :]
    qa = jnp.where(ids[:, None] == lane, 1.0, 0.0).astype(BF16)
    ka = jnp.where((lane >= 6) | (ids[:, None] == lane), 0.0, neg_large).astype(BF16)
    qxa = jnp.where(ids_x[:, None] == lane, 1.0, 0.0).astype(BF16)
    kxa = jnp.where((lane >= 6) | (ids_x[:, None] == lane), 0.0, neg_large).astype(BF16)
    hidden1, qkv = front(False, patch, mask_positions, table, w_qkv)
    unused, qkv_x = front(True, patch_x, mask_positions, table, w_qkv)
    attended, lse = attend(qkv, qkv_x, qa, ka, kxa)
    lse_rows = lse[:, :16].T
    lse_rows_x = lax.ppermute(lse_rows, "tm", swap)
    middle, hidden2, activated, grad_upper, up_sums = middle_part(
        patch, mask_positions, table, attended, w_out, cot, w_up, w_down, up_bias.astype(F32)[None]
    )
    parts, output, grad_patches, v = backward(
        (activated, cot, grad_upper, middle, hidden2, w_out, qkv, qkv_x, attended, hidden1, patch, w_qkv),
        (w_up, w_down),
        (qa, ka, qxa, kxa, lse_rows, lse_rows_x, table, mask_positions, up_sums),
    )
    grad_down, grad_up, grad_out, grad_qkv = widen(parts)
    return (
        output[None],
        grad_patches[None],
        v[0],
        v[1],
        v[2],
        grad_qkv,
        v[3],
        v[4],
        grad_out,
        v[5],
        v[6],
        v[7],
        grad_up,
        v[9:13].reshape(-1),
        grad_down,
        v[8],
    )


def shards(
    patches,
    segment_ids,
    mask_positions,
    mask_embed,
    norm1_gain,
    norm1_bias,
    w_qkv,
    query_bias,
    value_bias,
    w_out,
    out_bias,
    norm2_gain,
    norm2_bias,
    w_up,
    up_bias,
    w_down,
    down_bias,
    cotangent,
):
    rows_n, time_n, width = patches.shape
    query_scale = 1.0 / math.sqrt(HEAD)
    gain_one = norm1_gain.astype(jnp.float32)
    gain_two = norm2_gain.astype(jnp.float32)
    offset = lax.axis_index("tm") * time_n
    places = offset + lax.broadcasted_iota(jnp.int32, (rows_n, time_n, 1), 1)
    masked = jnp.any(places == mask_positions[:, None, :], axis=-1)[..., None]
    inputs = jnp.where(
        masked, mask_embed.astype(jnp.float32)[None, None, :], patches.astype(jnp.float32)
    )
    normed1, inverse1 = normalize(inputs)
    hidden1 = (normed1 * gain_one + norm1_bias.astype(jnp.float32)).astype(jnp.bfloat16)
    project = jnp.einsum("rtd,de->rte", hidden1, w_qkv, preferred_element_type=jnp.float32)
    queries = ((project[..., :width] + query_bias.astype(jnp.float32)) * query_scale).astype(
        jnp.bfloat16
    )
    keys_own = project[..., width : 2 * width].astype(jnp.bfloat16)
    values_own = (project[..., 2 * width :] + value_bias.astype(jnp.float32)).astype(jnp.bfloat16)
    keys_all, values_all, segments_all = (
        lax.all_gather(keys_own, "tm", axis=1, tiled=True),
        lax.all_gather(values_own, "tm", axis=1, tiled=True),
        lax.all_gather(segment_ids, "tm", axis=1, tiled=True),
    )
    same = segment_ids[:, :, None] == segments_all[:, None, :]
    query_heads = split_heads(queries)
    head_outputs, log_totals = attend_forward(
        query_heads, split_heads(keys_all), split_heads(values_all), same
    )
    attended = join_heads(head_outputs).astype(jnp.bfloat16)
    middle = (
        inputs
        + jnp.einsum("rtd,de->rte", attended, w_out, preferred_element_type=jnp.float32)
        + out_bias.astype(jnp.float32)
    )
    normed2, inverse2 = normalize(middle)
    hidden2 = (normed2 * gain_two + norm2_bias.astype(jnp.float32)).astype(jnp.bfloat16)
    upper = jnp.einsum(
        "rtd,df->rtf", hidden2, w_up, preferred_element_type=jnp.float32
    ) + up_bias.astype(jnp.float32)
    activated = jax.nn.gelu(upper, approximate=False).astype(jnp.bfloat16)
    result = (
        middle
        + jnp.einsum("rtf,fd->rtd", activated, w_down, preferred_element_type=jnp.float32)
        + down_bias.astype(jnp.float32)
    )
    output = result.astype(jnp.bfloat16)
    grad_result = cotangent.astype(jnp.float32)
    grad_w_down = jnp.einsum(
        "rtf,rtd->fd", activated, cotangent, preferred_element_type=jnp.float32
    )
    grad_down_bias = total_rows(grad_result)
    grad_activated = jnp.einsum(
        "rtd,fd->rtf", cotangent, w_down, preferred_element_type=jnp.float32
    )
    unused, gelu_pull = jax.vjp(partial(jax.nn.gelu, approximate=False), upper)
    grad_upper = gelu_pull(grad_activated)[0].astype(jnp.bfloat16)
    grad_w_up = jnp.einsum("rtd,rtf->df", hidden2, grad_upper, preferred_element_type=jnp.float32)
    grad_up_bias = total_rows(grad_upper)
    grad_hidden2 = jnp.einsum("rtf,df->rtd", grad_upper, w_up, preferred_element_type=jnp.float32)
    grad_gain_two = total_rows(grad_hidden2 * normed2)
    grad_bias_two = total_rows(grad_hidden2)
    grad_middle = grad_result + norm_back(grad_hidden2, normed2, inverse2, gain_two)
    mlp_vectors = jnp.stack([grad_gain_two, grad_bias_two, grad_down_bias], axis=1)
    grad_branch = grad_middle.astype(jnp.bfloat16)
    grad_w_out = jnp.einsum(
        "rtd,rte->de", attended, grad_branch, preferred_element_type=jnp.float32
    )
    grad_out_bias = total_rows(grad_branch)
    grad_attended = jnp.einsum(
        "rte,de->rtd", grad_branch, w_out, preferred_element_type=jnp.float32
    ).astype(jnp.bfloat16)
    keys_back, values_back, segments_back = (
        lax.all_gather(keys_own, "tm", axis=1, tiled=True),
        lax.all_gather(values_own, "tm", axis=1, tiled=True),
        lax.all_gather(segment_ids, "tm", axis=1, tiled=True),
    )
    same_back = segment_ids[:, :, None] == segments_back[:, None, :]
    grad_query_h, grad_keys_h, grad_values_h = attend_backward(
        query_heads,
        split_heads(keys_back),
        split_heads(values_back),
        split_heads(grad_attended),
        log_totals,
        same_back,
    )
    grad_keys, grad_values = (
        lax.psum_scatter(
            join_heads(grad_keys_h).astype(jnp.bfloat16), "tm", scatter_dimension=1, tiled=True
        ).astype(jnp.float32),
        lax.psum_scatter(
            join_heads(grad_values_h).astype(jnp.bfloat16), "tm", scatter_dimension=1, tiled=True
        ).astype(jnp.float32),
    )
    grad_queries = join_heads(grad_query_h).astype(jnp.bfloat16)
    grad_project = jnp.concatenate(
        [
            (grad_queries.astype(jnp.float32) * query_scale).astype(jnp.bfloat16),
            grad_keys.astype(jnp.bfloat16),
            grad_values.astype(jnp.bfloat16),
        ],
        axis=-1,
    )
    grad_w_qkv = jnp.einsum(
        "rtd,rte->de", hidden1, grad_project, preferred_element_type=jnp.float32
    )
    grad_query_bias = total_rows(grad_project[..., :width])
    grad_value_bias = total_rows(grad_project[..., 2 * width :])
    grad_hidden1 = jnp.einsum(
        "rte,de->rtd", grad_project, w_qkv, preferred_element_type=jnp.float32
    )
    grad_gain_one = total_rows(grad_hidden1 * normed1)
    grad_bias_one = total_rows(grad_hidden1)
    grad_inputs = grad_middle + norm_back(grad_hidden1, normed1, inverse1, gain_one)
    grad_mask = total_rows(jnp.where(masked, grad_inputs, 0.0))
    grad_patches = jnp.where(masked, 0.0, grad_inputs).astype(jnp.bfloat16)
    attn_vectors = jnp.stack(
        [grad_mask, grad_gain_one, grad_bias_one, grad_query_bias, grad_value_bias, grad_out_bias],
        axis=1,
    )
    every_part = (
        lax.psum_scatter(
            grad_w_qkv.astype(jnp.bfloat16), "tm", scatter_dimension=0, tiled=True
        ).astype(jnp.float32),
        lax.psum_scatter(
            grad_w_out.astype(jnp.bfloat16), "tm", scatter_dimension=0, tiled=True
        ).astype(jnp.float32),
        lax.psum_scatter(
            attn_vectors.astype(jnp.bfloat16), "tm", scatter_dimension=0, tiled=True
        ).astype(jnp.float32),
        lax.psum_scatter(
            grad_w_up.astype(jnp.bfloat16), "tm", scatter_dimension=0, tiled=True
        ).astype(jnp.float32),
        lax.psum_scatter(
            grad_w_down.astype(jnp.bfloat16), "tm", scatter_dimension=0, tiled=True
        ).astype(jnp.float32),
        lax.psum_scatter(
            mlp_vectors.astype(jnp.bfloat16), "tm", scatter_dimension=0, tiled=True
        ).astype(jnp.float32),
        lax.psum_scatter(
            grad_up_bias.astype(jnp.bfloat16), "tm", scatter_dimension=0, tiled=True
        ).astype(jnp.float32),
    )
    every_part = (
        lax.psum(every_part[0].astype(jnp.bfloat16), "rows").astype(jnp.float32),
        lax.psum(every_part[1].astype(jnp.bfloat16), "rows").astype(jnp.float32),
        lax.psum(every_part[2].astype(jnp.bfloat16), "rows").astype(jnp.float32),
        lax.psum(every_part[3].astype(jnp.bfloat16), "rows").astype(jnp.float32),
        lax.psum(every_part[4].astype(jnp.bfloat16), "rows").astype(jnp.float32),
        lax.psum(every_part[5].astype(jnp.bfloat16), "rows").astype(jnp.float32),
        lax.psum(every_part[6].astype(jnp.bfloat16), "rows").astype(jnp.float32),
    )
    summed_qkv, summed_out, summed_attn, summed_up, summed_down, summed_mlp, summed_up_bias = (
        every_part
    )
    return (
        output,
        grad_patches,
        summed_attn[:, 0],
        summed_attn[:, 1],
        summed_attn[:, 2],
        summed_qkv,
        summed_attn[:, 3],
        summed_attn[:, 4],
        summed_out,
        summed_attn[:, 5],
        summed_mlp[:, 0],
        summed_mlp[:, 1],
        summed_up,
        summed_up_bias,
        summed_down,
        summed_mlp[:, 2],
    )


def solution(mesh):
    placed = (
        P("rows", "tm", None),
        P("rows", "tm"),
        P("rows", None),
        P(),
        P(),
        P(),
        P(),
        P(),
        P(),
        P(),
        P(),
        P(),
        P(),
        P(),
        P(),
        P(),
        P(),
        P("rows", "tm", None),
    )
    return jax.shard_map(
        block_shards if dict(mesh.shape) == {"rows": 16, "tm": 2} else shards,
        mesh=mesh,
        in_specs=placed,
        out_specs=(
            P("rows", "tm", None),
            P("rows", "tm", None),
            P("tm"),
            P("tm"),
            P("tm"),
            P("tm", None),
            P("tm"),
            P("tm"),
            P("tm", None),
            P("tm"),
            P("tm"),
            P("tm"),
            P("tm", None),
            P("tm"),
            P("tm", None),
            P("tm"),
        ),
        check_vma=False,
    )
```

profile of v0, /device:TPU:0, one launch (start us, length us, event | category | flops | bytes accessed | tf_op | source)
XLA Modules:
  0.0 221.5 jit_solution(13552946269943077435)
XLA Ops:
  0.7 3.1 %collective-permute-start = (bf16[512,768]{1,0:T(8,128)(2,1)}, bf16[512,768]{1,0:T(8,128)(2,1)S(1)}, u32[]{:S(2)}, u32[]{:S(2)}) collective-permute-start(bf16[512,768]{1,0:T(8,128)(2,1)} %bitcast.13), channel_id=1, source_target_pairs={{0,1},{1,0},{2,3},{3,2},{4,5},{5,4},{6,7},{7,6},{8,9},{9,8},{10,11... | collective-permute-start | bytes 2359304 | tf_op jit(solution)/shard_map/ppermute | solution.py:882
  3.8 0.7 stack.27
  4.5 0.7 stack.28
  5.9 0.7 stack.30
  6.6 0.7 stack.31
  7.2 0.7 stack.32
  7.9 0.7 stack.33
  8.6 0.7 stack.34
  10.0 0.7 reshape.48
  11.4 6.7 %shard_map.297 = (bf16[512,768]{1,0:T(8,128)(2,1)}, bf16[512,2304]{1,0:T(8,128)(2,1)}) custom-call(bf16[512,768]{1,0:T(8,128)(2,1)} %bitcast.14, s32[1,409]{1,0:T(1,128)} %marks_ref.7, f32[16,768]{1,0:T(8,128)} %convert_element_type.16.table_ref, bf16[768,2304]{1,0:T(8,128)(2,1)} %wq_h.1), custom_call_target="tpu_custom_call" | custom-call | flops 1811939328 | bytes 8388608 | tf_op jit(solution)/shard_map/pallas_call | solution.py:174
  18.7 2.9 %collective-permute-done.1 = s32[512]{0:T(512)S(1)} collective-permute-done((s32[512]{0:T(512)}, s32[512]{0:T(512)S(1)}, u32[]{:S(2)}, u32[]{:S(2)}) %collective-permute-start.1) | collective-permute-done | bytes 2080 | tf_op jit(solution)/shard_map/ppermute | solution.py:884
  21.5 1.0 select_convert_fusion
  22.5 0.9 copy-done.6
  23.4 6.7 %shard_map.298 = (bf16[512,768]{1,0:T(8,128)(2,1)}, bf16[512,2304]{1,0:T(8,128)(2,1)}) custom-call(bf16[512,768]{1,0:T(8,128)(2,1)} %copy-done.6, s32[1,409]{1,0:T(1,128)} %marks_ref.7, f32[16,768]{1,0:T(8,128)} %convert_element_type.16.table_ref, bf16[768,2304]{1,0:T(8,128)(2,1)} %wq_h.1), custom_call_target="tpu_custom_call" | custom-call | flops 1811939328 | bytes 8388608 | tf_op jit(solution)/shard_map/pallas_call | solution.py:174
  30.1 14.2 %shard_map.299 = (bf16[512,768]{1,0:T(8,128)(2,1)}, f32[512,128]{1,0:T(8,128)}) custom-call(bf16[512,2304]{1,0:T(8,128)(2,1)} %get-tuple-element.34.q_ref.k_ref.v_ref.qkv_h, bf16[512,2304]{1,0:T(8,128)(2,1)} %get-tuple-element.34.q_ref.k_ref.v_ref.qkv_h, bf16[512,2304]{1,0:T(8,128)(2,1)} %get-tuple-element.34.q_ref.k_ref.v_ref.qkv_h, ...), custom_call_target="tpu_custom_call" | custom-call | flops 1610612736 | bytes 8388608 | tf_op jit(solution)/shard_map/pallas_call | solution.py:232
  44.3 1.1 copy.34
  45.4 1.8 collective-permute-start.2
  47.2 16.5 %shard_map.300 = (f32[512,768]{1,0:T(8,128)}, bf16[512,768]{1,0:T(8,128)(2,1)}, bf16[512,3072]{1,0:T(8,128)(2,1)}, bf16[512,3072]{1,0:T(8,128)(2,1)}, f32[1,3072]{1,0:T(1,128)}) custom-call(bf16[512,768]{1,0:T(8,128)(2,1)} %bitcast.15, s32[1,409]{1,0:T(1,128)} %marks_ref.7, f32[16,768]{1,0:T(8,128)} %convert_element_type.16.table_ref, ...), custom_call_target="tpu_custom_call" | custom-call | flops 5435817984 | bytes 25165824 | tf_op jit(solution)/shard_map/pallas_call | solution.py:305
  64.4 140.3 %shard_map.301 = (bf16[24,2,2,96,384]{4,3,2,1,0:T(8,128)(2,1)}, bf16[512,768]{1,0:T(8,128)(2,1)}, bf16[512,768]{1,0:T(8,128)(2,1)}, f32[16,384]{1,0:T(8,128)}) custom-call(bf16[512,3072]{1,0:T(8,128)(2,1)} %get-tuple-element.37.act_h, bf16[512,768]{1,0:T(8,128)(2,1)} %bitcast.18, bf16[512,3072]{1,0:T(8,128)(2,1)} %get-tuple-element.38.gu_h, ...), custom_call_target="tpu_custom_call" | custom-call | tf_op jit(solution)/shard_map/pallas_call | solution.py:767
  204.6 0.7 slice.42
  205.4 1.6 slice_reduce_fusion
  207.6 12.1 %shard_map.302 = (f32[1536,768]{1,0:T(8,128)}, f32[384,3072]{1,0:T(8,128)}, f32[384,768]{1,0:T(8,128)}, f32[384,2304]{1,0:T(8,128)}) custom-call(bf16[24,384,384]{2,1,0:T(8,128)(2,1)} %bitcast.9, bf16[24,384,384]{2,1,0:T(8,128)(2,1)} %bitcast.10), custom_call_target="tpu_custom_call" | custom-call | tf_op jit(solution)/shard_map/pallas_call | solution.py:836
  219.7 0.9 copy.37
  220.6 0.9 copy.38
  (25 shorter events, 4.0 us)
Async XLA Ops:
  0.6 20.9 %copy-start.5 = (s32[1,512]{1,0:T(1,128)S(1)}, s32[1,512]{1,0:T(1,128)}, u32[]{:S(2)}) copy-start(s32[1,512]{1,0:T(1,128)} %param.19) | copy-start | bytes 6148
  0.7 17.4 %copy-start.4 = (bf16[3072]{0:T(1024)(128)(2,1)S(1)}, bf16[3072]{0:T(1024)(128)(2,1)}, u32[]{:S(2)}) copy-start(bf16[3072]{0:T(1024)(128)(2,1)} %param.32) | copy-start | bytes 18436
  0.7 21.9 %collective-permute-start = (bf16[512,768]{1,0:T(8,128)(2,1)}, bf16[512,768]{1,0:T(8,128)(2,1)S(1)}, u32[]{:S(2)}, u32[]{:S(2)}) collective-permute-start(bf16[512,768]{1,0:T(8,128)(2,1)} %bitcast.13), channel_id=1, source_target_pairs={{0,1},{1,0},{2,3},{3,2},{4,5},{5,4},{6,7},{7,6},{8,9},{9,8},{10,11... | collective-permute-start | bytes 2359304 | tf_op jit(solution)/shard_map/ppermute | solution.py:882
  3.7 17.8 %collective-permute-start.1 = (s32[512]{0:T(512)}, s32[512]{0:T(512)S(1)}, u32[]{:S(2)}, u32[]{:S(2)}) collective-permute-start(s32[512]{0:T(512)} %bitcast.20), channel_id=1, source_target_pairs={{0,1},{1,0},{2,3},{3,2},{4,5},{5,4},{6,7},{7,6},{8,9},{9,8},{10,11... | collective-permute-start | bytes 6152 | tf_op jit(solution)/shard_map/ppermute | solution.py:884
  22.5 0.9 copy-start.6
  45.4 18.4 %copy-start.2 = (f32[16,512]{1,0:T(8,128)}, f32[16,512]{1,0:T(8,128)S(1)}, u32[]{:S(2)}) copy-start(f32[16,512]{1,0:T(8,128)S(1)} %slice_bitcast_fusion.lse_ref) | copy-start | bytes 98308
  45.4 18.4 %collective-permute-start.2 = (f32[16,512]{1,0:T(8,128)S(1)}, f32[16,512]{1,0:T(8,128)S(1)}, u32[]{:S(2)}, u32[]{:S(2)}) collective-permute-start(f32[16,512]{1,0:T(8,128)S(1)} %slice_bitcast_fusion.lse_ref), channel_id=1, source_target_pairs={{0,1},{1,0},{2,3},{3,2},{4,5},{5,4},{6,7},{7,6},{8,9},{9,8},{10,11... | collective-permute-start | bytes 98312 | tf_op jit(solution)/shard_map/ppermute | solution.py:913
  63.8 0.6 copy-start.3
  207.6 12.1 %copy-start.1 = (bf16[512,768]{1,0:T(8,128)(2,1)S(1)}, bf16[512,768]{1,0:T(8,128)(2,1)}, u32[]{:S(2)}) copy-start(bf16[512,768]{1,0:T(8,128)(2,1)} %get-tuple-element.44) | copy-start | bytes 2359300
  207.6 13.0 %copy-start = (bf16[512,768]{1,0:T(8,128)(2,1)S(1)}, bf16[512,768]{1,0:T(8,128)(2,1)}, u32[]{:S(2)}) copy-start(bf16[512,768]{1,0:T(8,128)(2,1)} %get-tuple-element.45) | copy-start | bytes 2359300
where the time goes:
time: 223 us; the launch traced here: 221 us
  Pallas kernels  196 us (88%)
  local copies, waits for them, and re-layouts  14.2 us (6%)
  starting transfers between devices  4.94 us (2%)
  waiting for transfers between devices  2.86 us (1%)
    pallas_call x1, Pallas kernels, backward(): pl.pallas_call(halves_kernel, out_shape=(jax.ShapeDtypeStruct((CHUNKS, 2,...  140 us
    pallas_call x1, Pallas kernels, middle_part(): pl.pallas_call(middle_kernel, grid=(3072 // FF_TILE,), out_shape=(jax.Sha...  16.5 us
    pallas_call x1, Pallas kernels, attend(): pl.pallas_call(attend_kernel, grid=(6,), out_shape=(jax.ShapeDtypeStruct(...  14.2 us
    pallas_call x2, Pallas kernels, front(): pl.pallas_call(partial(front_kernel, other), grid=(HALF // TILE,), out_sh...  13.4 us
    pallas_call x1, Pallas kernels, widen(): pl.pallas_call(widen_kernel, grid=(12,), out_shape=(jax.ShapeDtypeStruct(...  12.1 us
    another operation x9, local copies, waits for them, and re-layouts, block_shards(): jnp.stack([mask_embed, norm1_gain, norm1_bias, query_bias, value_bias, ou...  6.16 us
  transfers between devices with their start and end apart: 3, of which 1 were waited for; matrix products, arithmetic and copies ran while one was open for 4% of the time, Pallas kernels for 10%

commit v1 on v0

--- a/solution.py
+++ b/solution.py
@@ -88,7 +88,7 @@
 MESH = pl.DeviceIdType.MESH
 SUB = 96
 COLS = 384
-LAGS = (0, 1, 3, 4, 5, 7, 8, 9)
+LAGS = (0, 1, 5, 6, 7, 9, 11, 12)
 
 
 def places():
@@ -140,6 +140,23 @@
     return lax.dot_general(a, b, (((0,), (0,)), ((), ())), preferred_element_type=F32)
 
 
+def table_kernel(*refs):
+    table_ref = refs[-1]
+    table_ref[...] = jnp.zeros_like(table_ref)
+    for i, ref in enumerate(refs[:-1]):
+        table_ref[i : i + 1, :] = ref[...].astype(F32).reshape(1, 768)
+
+
+def tabulate(smalls):
+    near = pl.BlockSpec(memory_space=pltpu.VMEM)
+    return pl.pallas_call(
+        table_kernel,
+        out_shape=jax.ShapeDtypeStruct((16, 768), F32),
+        in_specs=[near] * len(smalls),
+        out_specs=near,
+    )(*smalls)
+
+
 def standard(values):
     center = values - jnp.mean(values, axis=-1, keepdims=True)
     scale_inv = lax.rsqrt(jnp.mean(center * center, axis=-1, keepdims=True) + norm_eps)
@@ -152,13 +169,10 @@
     return flagged, jnp.where(flagged, embed, patch.astype(F32))
 
 
-def front_kernel(other, p_ref, marks_ref, table_ref, w_ref, h1_ref, qkv_ref):
-    y = lax.axis_index("tm")
-    first = (1 - y if other else y) * HALF + pl.program_id(0) * TILE
-    unused, inputs = masked_inputs(p_ref[...], first, marks_ref[...], table_ref[R_EMBED : R_EMBED + 1, :])
+def project_tile(patch, first, marks_ref, table_ref, w_ref, qkv_ref):
+    unused, inputs = masked_inputs(patch, first, marks_ref[...], table_ref[R_EMBED : R_EMBED + 1, :])
     normed, unused = standard(inputs)
     hidden = (normed * table_ref[R_G1 : R_G1 + 1, :] + table_ref[R_B1 : R_B1 + 1, :]).astype(BF16)
-    h1_ref[...] = hidden
     for part in range(6):
         cols = slice(part * 384, part * 384 + 384)
         project = dot(hidden, w_ref[:, cols])
@@ -168,77 +182,105 @@
         elif part >= 4:
             project = project + table_ref[R_VB : R_VB + 1, bias]
         qkv_ref[:, cols] = project.astype(BF16)
-
-
-def front(other, patch, marks, table, w_qkv):
+    return hidden
+
+
+def own_kernel(p_ref, marks_ref, table_ref, w_ref, qkv_ref, h1_ref):
+    first = lax.axis_index("tm") * HALF + pl.program_id(0) * TILE
+    h1_ref[...] = project_tile(p_ref[...], first, marks_ref, table_ref, w_ref, qkv_ref)
+
+
+def other_kernel(near, p_ref, marks_ref, table_ref, w_ref, qkv_ref):
+    y = lax.axis_index("tm")
+    first = (1 - y) * HALF + (y if near else 1 - y) * TILE
+    project_tile(p_ref[...], first, marks_ref, table_ref, w_ref, qkv_ref)
+
+
+def front(kernel, patch, marks, table, w_qkv):
+    own = patch.shape[0] == HALF
+    length = HALF if own else TILE
+    widths = (2304, 768) if own else (2304,)
     return pl.pallas_call(
-        partial(front_kernel, other),
-        grid=(HALF // TILE,),
-        out_shape=(
-            jax.ShapeDtypeStruct((HALF, 768), BF16),
-            jax.ShapeDtypeStruct((HALF, 2304), BF16),
-        ),
+        kernel,
+        grid=(length // TILE,),
+        out_shape=tuple(jax.ShapeDtypeStruct((length, n), BF16) for n in widths),
         in_specs=[
             pl.BlockSpec((TILE, 768), lambda i: (i, 0)),
             pl.BlockSpec(marks.shape, lambda i: (0, 0)),
             pl.BlockSpec(table.shape, lambda i: (0, 0)),
             pl.BlockSpec((768, 2304), lambda i: (0, 0), pipeline_mode=pl.Buffered(1)),
         ],
-        out_specs=(
-            pl.BlockSpec((TILE, 768), lambda i: (i, 0)),
-            pl.BlockSpec((TILE, 2304), lambda i: (i, 0)),
-        ),
-        cost_estimate=pl.CostEstimate(flops=2 * HALF * 768 * 2304, bytes_accessed=8 << 20, transcendentals=0),
+        out_specs=tuple(pl.BlockSpec((TILE, n), lambda i: (i, 0)) for n in widths),
+        cost_estimate=pl.CostEstimate(flops=2 * length * 768 * 2304, bytes_accessed=8 << 20, transcendentals=0),
     )(patch, marks, table, w_qkv)
 
 
-def attend_kernel(q_ref, k_ref, v_ref, kx_ref, vx_ref, qa_ref, ka_ref, kxa_ref, o_ref, lse_ref):
+def attend_kernel(
+    q_ref, k_ref, v_ref, kn_ref, vn_ref, kf_ref, vf_ref, qa_ref, ka_ref, kxa_ref, on_ref, of_ref, ln_ref, lf_ref, marks_ref
+):
     y = lax.axis_index("tm")
     pair = pl.program_id(0)
     lane = lax.broadcasted_iota(jnp.int32, (1, 128), 1)
-    keys = jnp.concatenate([k_ref[...], ka_ref[...]], axis=1)
-    far_keys = jnp.concatenate([kx_ref[...], kxa_ref[...]], axis=1)
-    near_x = pl.multiple_of(y * TILE, TILE)
-    near_keys = jnp.concatenate([kx_ref[pl.ds(near_x, TILE), :], kxa_ref[pl.ds(near_x, TILE), :]], axis=1)
-    for far in range(2):
-        rows = pl.ds(pl.multiple_of((y if far else 1 - y) * TILE, TILE), TILE)
+
+    def rows_of(index):
+        return pl.ds(pl.multiple_of(index * TILE, TILE), TILE)
+
+    blocks = [
+        (k_ref, ka_ref[...], v_ref),
+        (kn_ref, kxa_ref[rows_of(y), :], vn_ref),
+        (kf_ref, kxa_ref[rows_of(1 - y), :], vf_ref),
+    ]
+    all_keys = [jnp.concatenate([k[...], a], axis=1) for k, a, unused in blocks]
+    for far, number, o_ref, lse_ref in ((0, 3, on_ref, ln_ref), (1, 2, of_ref, lf_ref)):
+        rows = rows_of(y if far else 1 - y)
         q = q_ref[rows, :]
         qa = qa_ref[rows, :]
         kept = None
-        marks = jnp.where(pair == 0, 0.0, lse_ref[rows, :])
+        marks = jnp.where(pair == 0, 0.0, marks_ref[far])
         for h in range(2):
             mine = (lane // 64) == h
             query = jnp.concatenate([jnp.where(mine, q, 0), qa], axis=1)
-            own = dot_t(query, keys)
-            cross = dot_t(query, near_keys if far else far_keys)
-            peak = jnp.maximum(jnp.max(own, axis=-1, keepdims=True), jnp.max(cross, axis=-1, keepdims=True))
-            own = jnp.exp(own - peak)
-            cross = jnp.exp(cross - peak)
-            total = jnp.sum(own, axis=-1, keepdims=True) + jnp.sum(cross, axis=-1, keepdims=True)
-            values = vx_ref[pl.ds(near_x, TILE), :] if far else vx_ref[...]
-            out = dot(own.astype(BF16), v_ref[...]) + dot(cross.astype(BF16), values)
+            scores = [dot_t(query, key) for key in all_keys[:number]]
+            peak = jnp.max(scores[0], axis=-1, keepdims=True)
+            for more in scores[1:]:
+                peak = jnp.maximum(peak, jnp.max(more, axis=-1, keepdims=True))
+            total = 0.0
+            out = 0.0
+            for score, block in zip(scores, blocks):
+                weights = jnp.exp(score - peak)
+                total = total + jnp.sum(weights, axis=-1, keepdims=True)
+                out = out + dot(weights.astype(BF16), block[2][...])
             out = out / total
             kept = out if h == 0 else jnp.where(mine, out, kept)
             marks = jnp.where(lane == 2 * pair + h, peak + jnp.log(total), marks)
-        o_ref[rows, :] = kept.astype(BF16)
-        lse_ref[rows, :] = marks
-
-
-def attend(qkv, qkv_other, qa, ka, kxa):
-    def block(first):
-        return pl.BlockSpec((HALF, 128), lambda i: (0, first + i))
+        o_ref[...] = kept.astype(BF16)
+        marks_ref[far] = marks
+
+    @pl.when(pair == 5)
+    def _():
+        ln_ref[...] = marks_ref[0].T[:16, :]
+        lf_ref[...] = marks_ref[1].T[:16, :]
+
+
+def attend(qkv, near, far, qa, ka, kxa):
+    def block(first, length):
+        return pl.BlockSpec((length, 128), lambda i: (0, first + i))
 
     whole = pl.BlockSpec((HALF, 128), lambda i: (0, 0))
+    stat = pl.BlockSpec((16, TILE), lambda i: (0, 0))
     return pl.pallas_call(
         attend_kernel,
         grid=(6,),
-        out_shape=(jax.ShapeDtypeStruct((HALF, 768), BF16), jax.ShapeDtypeStruct((HALF, 128), F32)),
-        in_specs=[block(0), block(6), block(12), block(6), block(12), whole, whole, whole],
-        out_specs=(pl.BlockSpec((HALF, 128), lambda i: (0, i)), whole),
+        out_shape=(jax.ShapeDtypeStruct((TILE, 768), BF16),) * 2 + (jax.ShapeDtypeStruct((16, TILE), F32),) * 2,
+        in_specs=[block(0, HALF), block(6, HALF), block(12, HALF)]
+        + [block(6, TILE), block(12, TILE)] * 2
+        + [whole] * 3,
+        out_specs=(block(0, TILE), block(0, TILE), stat, stat),
+        scratch_shapes=[pltpu.VMEM((2, TILE, 128), F32)],
         cost_estimate=pl.CostEstimate(
             flops=4 * 12 * HALF * 1024 * 64, bytes_accessed=8 << 20, transcendentals=12 * HALF * 1024
         ),
-    )(qkv, qkv, qkv, qkv_other, qkv_other, qa, ka, kxa)
+    )(qkv, qkv, qkv, near, near, far, far, qa, ka, kxa)
 
 
 ERFC_P = 0.3275911
@@ -265,120 +307,65 @@
     return u * phi, phi + u * (bell * (1.0 / math.sqrt(2.0 * math.pi)))
 
 
+CHUNKS = 24
+SLOTS = 5
 FF_TILE = 384
-
-
-def middle_kernel(
-    p_ref, marks_ref, table_ref, a_ref, wo_ref, cot_ref, wu_ref, wd_ref, ub_ref, mid_ref, h2_ref, act_ref, gu_ref, ubs_ref
-):
-    y = lax.axis_index("tm")
-
-    @pl.when(pl.program_id(0) == 0)
-    def _():
-        for tile in range(HALF // TILE):
-            rows = slice(tile * TILE, tile * TILE + TILE)
-            unused, inputs = masked_inputs(
-                p_ref[rows, :], y * HALF + tile * TILE, marks_ref[...], table_ref[R_EMBED : R_EMBED + 1, :]
-            )
-            mid = inputs + dot(a_ref[rows, :], wo_ref[...]) + table_ref[R_OB : R_OB + 1, :]
-            normed, unused = standard(mid)
-            mid_ref[rows, :] = mid
-            h2_ref[rows, :] = (normed * table_ref[R_G2 : R_G2 + 1, :] + table_ref[R_B2 : R_B2 + 1, :]).astype(BF16)
-
-    sums = jnp.zeros((1, FF_TILE), F32)
-    for tile in range(HALF // TILE):
-        rows = slice(tile * TILE, tile * TILE + TILE)
-        upper = dot(h2_ref[rows, :], wu_ref[...]) + ub_ref[...]
-        value, slope = gelu_and_slope(upper)
-        act_ref[rows, :] = value.astype(BF16)
-        grad = dot_t(cot_ref[rows, :], wd_ref[...])
-        low = (grad * slope).astype(BF16)
-        gu_ref[rows, :] = low
-        sums = sums + jnp.sum(low.astype(F32), axis=0, keepdims=True)
-    ubs_ref[...] = sums
-
-
-def middle_part(patch, marks, table, attended, w_out, cot, w_up, w_down, up_bias):
-    def full(shape):
-        return pl.BlockSpec(shape, lambda i: (0, 0))
-
-    return pl.pallas_call(
-        middle_kernel,
-        grid=(3072 // FF_TILE,),
-        out_shape=(
-            jax.ShapeDtypeStruct((HALF, 768), F32),
-            jax.ShapeDtypeStruct((HALF, 768), BF16),
-            jax.ShapeDtypeStruct((HALF, 3072), BF16),
-            jax.ShapeDtypeStruct((HALF, 3072), BF16),
-            jax.ShapeDtypeStruct((1, 3072), F32),
-        ),
-        in_specs=[
-            full((HALF, 768)),
-            full(marks.shape),
-            full(table.shape),
-            full((HALF, 768)),
-            full((768, 768)),
-            full((HALF, 768)),
-            pl.BlockSpec((768, FF_TILE), lambda i: (0, i)),
-            pl.BlockSpec((FF_TILE, 768), lambda i: (i, 0)),
-            pl.BlockSpec((1, FF_TILE), lambda i: (0, i)),
-        ],
-        out_specs=(
-            full((HALF, 768)),
-            full((HALF, 768)),
-            pl.BlockSpec((HALF, FF_TILE), lambda i: (0, i)),
-            pl.BlockSpec((HALF, FF_TILE), lambda i: (0, i)),
-            pl.BlockSpec((1, FF_TILE), lambda i: (0, i)),
-        ),
-        cost_estimate=pl.CostEstimate(
-            flops=2 * HALF * 768 * (768 + 6144), bytes_accessed=24 << 20, transcendentals=HALF * 3072
-        ),
-    )(patch, marks, table, attended, w_out, cot, w_up, w_down, up_bias)
-
-
-CHUNKS = 24
-T_OWN = 6
-T_LAST = 24
-T_VEC = 28
+T_FORWARD = (0, 0, 1, 2, 3, 4, 5, 6)
+EMIT_DOWN, EMIT_UP, EMIT_OUT, EMIT_QKV = (0, 2, 4, 6), (8, 10, 12, 14), (16,), (18, 19, 20, 21, 22, 23)
+T_SECOND, T_ATTENDED = (7,), (8,)
+T_SEND = (8, 9, 9, 10, 11, 11, 12, 13, 13, 14, 15, 15)
+T_OWN = (8, 9, 10, 13, 14, 15)
+T_FAR = (12, 13, 14, 16, 17, 18)
+T_OUTPUT = (19, 19, 20, 20, 21, 21, 22, 22)
+T_GRAD = (24, 24, 25)
+T_FIRST = (26,)
+T_VEC = 27
 
 
 def halves_kernel(
-    act_h, cot_h, gu_h, mid_h, h2_h, wo_h, qkv_h, qkvx_h, att_h, h1_h, patch_h, wq_h, wu_h, wd_h,
-    qa_ref, ka_ref, qxa_ref, kxa_ref, lse_ref, lsex_ref, table_ref, marks_ref, ub_ref,
+    cot_h, wo_h, qkv_h, h1_h, patch_h, wq_h, otn_h, otf_h, atn_h, atf_h, wu_h, wd_h,
+    qa_ref, ka_ref, qxa_ref, kxa_ref, lsen_ref, lsef_ref, table_ref, marks_ref, ub_ref,
     parts_h, out_h, gp_h, vec_out,
-    act, cot, gu, mid, h2, wo, qkv, qkvx, att, h1, patch, wq, wu, wd,
-    acc, gb, do, dox, dqkv, dq, dk, dv, drow, dxrow,
+    cot, wo, qkv, h1, patch, wq, qkvx, att, wu, wd,
+    act, gu, mid, h2, acc, gb, do, dox, dqkv, dq, dk, dv, drow, dxrow, lse_ref, lsex_ref,
     g, r1, r2, r3, r4, r5, done, v0, v1, v2,
     insem, wusem, wdsem, ssem, rsem, vs, vr, xs, xr, outsem, lastsem,
 ):
     core, x, y, peers = places()
     pair, yp, xp, zp1, zp2 = peers
     lane = lax.broadcasted_iota(jnp.int32, (1, 128), 1)
+    near_rows = pl.ds(pl.multiple_of((1 - y) * TILE, TILE), TILE)
+    far_rows = pl.ds(pl.multiple_of(y * TILE, TILE), TILE)
     inputs = (
-        (act_h, act), (cot_h, cot), (gu_h, gu), (mid_h, mid), (h2_h, h2), (wo_h, wo),
-        (qkv_h, qkv), (att_h, att), (qkvx_h, qkvx), (h1_h, h1), (patch_h, patch), (wq_h, wq),
-    )
-    ACT, COT, GU, MID, H2, WO, QKV, ATT, QKVX, H1, PATCH, WQ = range(12)
+        (cot_h, cot), (wo_h, wo), (qkv_h, qkv), (h1_h, h1), (patch_h, patch), (wq_h, wq),
+        (otn_h, qkvx.at[far_rows, :]), (otf_h, qkvx.at[near_rows, :]),
+        (atn_h, att.at[near_rows, :]), (atf_h, att.at[far_rows, :]),
+    )
+    COT, WO, QKV, H1, PATCH, WQ, OTN, OTF, ATN, ATF = range(10)
+
+    def lanes(start, size=128):
+        return pl.ds(pl.multiple_of(start, 128), size)
+
+    def part_of(n):
+        return (n // 2 + 4 * (n % 2)) * (1 - n // 8) + (n - 8) * (n // 8)
 
     def load(i):
         return pltpu.make_async_copy(inputs[i][0], inputs[i][1], insem.at[i])
 
-    def up_tile(k):
-        cols = pl.ds(pl.multiple_of(k * 512, 512), 512)
-        return pltpu.make_async_copy(wu_h.at[:, cols], wu.at[k % 2], wusem.at[k % 2])
-
-    def down_tile(k):
-        rows = pl.ds(pl.multiple_of(k * 512, 512), 512)
-        return pltpu.make_async_copy(wd_h.at[rows, :], wd.at[k % 2], wdsem.at[k % 2])
-
-    for i in (ACT, COT, GU):
+    def up_tile(n):
+        return pltpu.make_async_copy(wu_h.at[:, lanes(part_of(n) * FF_TILE, FF_TILE)], wu.at[n % 2], wusem.at[n % 2])
+
+    def down_tile(n):
+        rows = pl.ds(pl.multiple_of(part_of(n) * FF_TILE, FF_TILE), FF_TILE)
+        return pltpu.make_async_copy(wd_h.at[rows, :], wd.at[n % 2], wdsem.at[n % 2])
+
+    for i in (PATCH, WO, ATN, ATF):
         load(i).start()
-    up_tile(0).start()
-    up_tile(1).start()
-    for i in (MID, H2, WO, QKV, ATT, QKVX, H1, PATCH, WQ):
+    for n in range(2):
+        up_tile(n).start()
+        down_tile(n).start()
+    for i in (COT, QKV, OTN, OTF, H1, WQ):
         load(i).start()
-    down_tile(0).start()
-    down_tile(1).start()
     greet(peers)
 
     def remote(src, dst, send, recv, dev):
@@ -388,7 +375,7 @@
 
     def copy(s, c):
         src, dst, dev = (
-            lambda: (g.at[c % 4, 1 - core], r1.at[c], pair),
+            lambda: (g.at[c % SLOTS, 1 - core], r1.at[c], pair),
             lambda: (r1.at[c, 1 - y], r2.at[c], yp),
             lambda: (r2.at[c, 1 - x], r3.at[c], xp),
             lambda: (r3.at[c], r4.at[c], zp1),
@@ -405,7 +392,7 @@
         if s > 0:
             copy(s - 1, c).wait_recv()
         if s == 1:
-            r1[c] = r1[c] + g[c % 4, core]
+            r1[c] = r1[c] + g[c % SLOTS, core]
         elif s == 2:
             r2[c] = r2[c] + r1[c, y]
         elif s == 3:
@@ -446,8 +433,12 @@
             vec_copy(s).start()
 
     def far_copy(i):
-        src, dst = ((do, dox), (drow, dxrow))[i]
+        src, dst = ((lse_ref, lsex_ref), (drow, dxrow))[i]
         return remote(src, dst, xs.at[i], xr.at[i], yp)
+
+    def grad_copy(n):
+        rows, cols = pl.ds(pl.multiple_of((n % 2) * TILE, TILE), TILE), lanes((n // 2) * 128)
+        return remote(do.at[rows, cols], dox.at[rows, cols], xs.at[2 + n], xr.at[2 + n], yp)
 
     def row(r):
         return table_ref[r : r + 1, :]
@@ -460,29 +451,46 @@
         number = right.shape[1] // 384
         for i in range(number):
 
-            @pl.when(c + i >= 4)
+            @pl.when(c + i >= SLOTS)
             def _():
-                copy(0, c + i - 4).wait_send()
+                copy(0, c + i - SLOTS).wait_send()
 
         for half in range(2):
             block = t_dot(left(half), right).astype(BF16)
             for i in range(number):
                 for other in range(4):
                     rows = slice(other * SUB, other * SUB + SUB)
-                    g[(c + i) % 4, other // 2, half, other % 2] = block[rows, i * 384 : i * 384 + 384]
-
-    def lanes(start, size=128):
-        return pl.ds(pl.multiple_of(start, 128), size)
-
-    def grad_hidden(k):
-        up_tile(k).wait()
-        for tile in range(2):
-            rows = slice(tile * 256, tile * 256 + 256)
-            acc[rows, :] = acc[rows, :] + dot_t(gu[rows, lanes(k * 512, 512)], wu[k % 2])
-
-        @pl.when(k + 2 < 6)
+                    g[(c + i) % SLOTS, other // 2, half, other % 2] = block[rows, i * 384 : i * 384 + 384]
+
+    def enter():
+        for tile in range(HALF // TILE):
+            rows = slice(tile * TILE, tile * TILE + TILE)
+            unused, values = masked_inputs(patch[rows, :], y * HALF + tile * TILE, marks_ref[...], row(R_EMBED))
+            total = values + dot(att[rows, :], wo[...]) + row(R_OB)
+            normed, unused = standard(total)
+            mid[rows, :] = total
+            h2[rows, :] = (normed * row(R_G2) + row(R_B2)).astype(BF16)
+
+    def forward(n):
+        k = part_of(n)
+        cols = lanes(k * FF_TILE, FF_TILE)
+        up_tile(n).wait()
+        down_tile(n).wait()
+        sums = jnp.zeros((1, FF_TILE), F32)
+        for tile in range(HALF // TILE):
+            rows = slice(tile * TILE, tile * TILE + TILE)
+            value, slope = gelu_and_slope(dot(h2[rows, :], wu[n % 2]) + ub_ref[:, cols])
+            act[rows, cols] = value.astype(BF16)
+            low = (dot_t(cot[rows, :], wd[n % 2]) * slope).astype(BF16)
+            gu[rows, cols] = low
+            sums = sums + jnp.sum(low.astype(F32), axis=0, keepdims=True)
+            acc[rows, :] = acc[rows, :] + dot_t(low, wu[n % 2])
+        v0[k // 4, pl.ds(9 + k % 4, 1), :] = sums
+        down_tile(n + 2).start()
+
+        @pl.when(n + 2 < 8)
         def _():
-            up_tile(k + 2).start()
+            up_tile(n + 2).start()
 
     def second_norm():
         def tile(i, carry):
@@ -516,7 +524,6 @@
                     total = jnp.sum(jnp.where((lane // 64) == h, product, 0.0), axis=1, keepdims=True)
                     columns = jnp.where(lane == 2 * p + h, total, columns)
             drow[:, rows] = columns.T[:16, :]
-        far_copy(0).start()
         far_copy(1).start()
 
     def piece(keys, key_mask, values, query, query_mask, grad, lse, delta):
@@ -552,6 +559,8 @@
 
     def far_pair(p):
         slot = p % 3
+        grad_copy(2 * p).wait_recv()
+        grad_copy(2 * p + 1).wait_recv()
         near, far = pl.multiple_of((1 - y) * 256, 256), pl.multiple_of(y * 256, 256)
 
         def head(h, carry):
@@ -584,15 +593,16 @@
         dqkv[:, lanes(768 + p * 128)] = dk[slot].astype(BF16)
         dqkv[:, lanes(1536 + p * 128)] = dv[slot].astype(BF16)
 
-    def output_tile(k):
-        down_tile(k).wait()
+    def output_tile(i):
+        n = i + 8
+        down_tile(n).wait()
         for tile in range(2):
             rows = slice(tile * 256, tile * 256 + 256)
-            mid[rows, :] = mid[rows, :] + dot(act[rows, lanes(k * 512, 512)], wd[k % 2])
-
-        @pl.when(k + 2 < 6)
+            mid[rows, :] = mid[rows, :] + dot(act[rows, lanes(i * FF_TILE, FF_TILE)], wd[n % 2])
+
+        @pl.when(n + 2 < 16)
         def _():
-            down_tile(k + 2).start()
+            down_tile(n + 2).start()
 
     def store_output():
         for tile in range(4):
@@ -624,37 +634,50 @@
         lax.fori_loop(0, 4, tile, 0)
         pltpu.make_async_copy(att, gp_h, lastsem.at[1]).start()
 
+    lse_ref[:, near_rows] = lsen_ref[...]
+    lse_ref[:, far_rows] = lsef_ref[...]
+    far_copy(0).start()
     acc[...] = jnp.zeros_like(acc)
     v0[...] = jnp.zeros_like(v0)
-    for half in range(2):
-        for i in range(4):
-            start = half * 1536 + i * 384
-            v0[half, 9 + i : 10 + i, :] = ub_ref[:, start : start + 384]
-    load(ACT).wait()
+    for i in (PATCH, WO, ATN, ATF):
+        load(i).wait()
+    enter()
     load(COT).wait()
 
     def step(t, carry):
-        even = t % 2 == 0
-
-        @pl.when((t < 8) & even)
-        def _():
-            start = t * 192
-            emit(lambda half: act[:, lanes(half * 1536 + start, 384)], cot[...], t)
-
-        @pl.when((t >= 8) & (t < 16) & even)
-        def _():
-            emit(lambda half: h2[:, half * 384 : half * 384 + 384], gu[:, lanes((t - 8) * 384, 768)], t)
-
-        @pl.when(t == 16)
-        def _():
-            emit(lambda half: att[:, half * 384 : half * 384 + 384], gb[...], t)
-
-        @pl.when((t >= 18) & (t < 24))
-        def _():
-            p = t - 18
+        def run(times, body):
+            def before(now):
+                return sum(jnp.where(now > at, 1, 0) for at in times)
+
+            def one(n, inner):
+                body(n)
+                return inner
+
+            lax.fori_loop(before(t), before(t + 1), one, 0)
+
+        def need(at, *names):
+            @pl.when(t == at)
+            def _():
+                for i in names:
+                    load(i).wait()
+
+        need(2, QKV, OTN, OTF, H1, WQ)
+        run(T_FORWARD, forward)
+        run(
+            EMIT_DOWN,
+            lambda n: emit(lambda half: act[:, lanes(half * 1536 + n * 384, 384)], cot[...], 2 * n),
+        )
+        run(
+            EMIT_UP,
+            lambda n: emit(lambda half: h2[:, half * 384 : half * 384 + 384], gu[:, lanes(n * 768, 768)], 8 + 2 * n),
+        )
+        run(EMIT_OUT, lambda n: emit(lambda half: att[:, half * 384 : half * 384 + 384], gb[...], 16))
+
+        def emit_qkv(p):
             right = jnp.concatenate([dqkv[:, lanes(part * 768 + p * 128)] for part in range(3)], axis=1)
-            emit(lambda half: h1[:, half * 384 : half * 384 + 384], right, t)
-
+            emit(lambda half: h1[:, half * 384 : half * 384 + 384], right, 18 + p)
+
+        run(EMIT_QKV, emit_qkv)
         for s in range(2):
             c = t - LAGS[s]
 
@@ -662,61 +685,25 @@
             def _():
                 stage(s, c)
 
-        @pl.when(t == 0)
-        def _():
-            load(GU).wait()
-
-        @pl.when(t < 3)
-        def _():
-            grad_hidden(2 * t)
-            grad_hidden(2 * t + 1)
-
-        @pl.when(t == 3)
-        def _():
-            load(MID).wait()
-            second_norm()
-
-        @pl.when(t == 4)
-        def _():
-            for i in (WO, ATT):
-                load(i).wait()
-            grad_attended()
-
-        u = t - T_OWN
-
-        @pl.when(u == 0)
-        def _():
-            for i in (H2, QKV, QKVX, H1, PATCH, WQ):
-                load(i).wait()
-
-        @pl.when((u >= 0) & ((u <= 2) | ((u <= 8) & (u % 2 == 0))))
-        def _():
-            own_pair(jnp.where(u <= 2, u, (u + 2) // 2))
-
-        @pl.when(u == 3)
+        run(T_SECOND, lambda n: second_norm())
+        run(T_ATTENDED, lambda n: grad_attended())
+        run(T_SEND, lambda n: grad_copy(n).start())
+        run(T_OWN, own_pair)
+
+        @pl.when(t == T_FAR[0])
         def _():
             far_copy(0).wait_recv()
             far_copy(1).wait_recv()
 
-        @pl.when((u >= 3) & (u <= 11) & ((u >= 10) | (u % 2 == 1)))
-        def _():
-            far_pair(jnp.where(u <= 9, (u - 3) // 2, u - 6))
-
-        @pl.when((t >= 18) & (t < 24))
-        def _():
-            output_tile(t - 18)
-
-        @pl.when(t == 23)
+        run(T_FAR, far_pair)
+        run(T_OUTPUT, output_tile)
+
+        @pl.when(t == T_OUTPUT[-1])
         def _():
             store_output()
 
-        @pl.when((t >= T_LAST) & (t < T_LAST + 3))
-        def _():
-            grad_first(t - T_LAST)
-
-        @pl.when(t == T_LAST + 3)
-        def _():
-            first_norm()
+        run(T_GRAD, grad_first)
+        run(T_FIRST, lambda n: first_norm())
 
         for s in range(2, 8):
             c = t - LAGS[s]
@@ -733,7 +720,7 @@
 
         return carry
 
-    lax.fori_loop(0, T_VEC + 6, step, 0)
+    lax.fori_loop(0, max(T_VEC + 6, CHUNKS + LAGS[7]), step, 0)
 
     def drain(c, carry):
         for s in range(1, 5):
@@ -742,12 +729,18 @@
         return carry
 
     lax.fori_loop(0, CHUNKS, drain, 0)
-    for c in range(CHUNKS - 4, CHUNKS):
+    for c in range(CHUNKS - SLOTS, CHUNKS):
         copy(0, c).wait_send()
     for s in range(5):
         vec_copy(s).wait_send()
     for i in range(2):
         far_copy(i).wait_send()
+
+    def drain_grad(n, carry):
+        grad_copy(n).wait_send()
+        return carry
+
+    lax.fori_loop(0, 12, drain_grad, 0)
     pltpu.make_async_copy(gb, out_h, lastsem.at[0]).wait()
     pltpu.make_async_copy(att, gp_h, lastsem.at[1]).wait()
 
@@ -763,7 +756,7 @@
         return pltpu.VMEM(shape, F32)
 
     dma = pltpu.SemaphoreType.DMA
-    held = [pltpu.VMEM(a.shape, a.dtype) for a in big]
+    held = [pltpu.VMEM(a.shape, a.dtype) for a in big[:6]] + [low(HALF, 2304), low(HALF, 768)]
     return pl.pallas_call(
         halves_kernel,
         out_shape=(
@@ -776,8 +769,12 @@
         out_specs=(hbm, hbm, hbm, near),
         scratch_shapes=held
         + [
-            low(2, 768, 512),
-            low(2, 512, 768),
+            low(2, 768, FF_TILE),
+            low(2, FF_TILE, 768),
+            low(HALF, 3072),
+            low(HALF, 3072),
+            full(HALF, 768),
+            low(HALF, 768),
             full(HALF, 768),
             low(HALF, 768),
             low(HALF, 768),
@@ -788,7 +785,9 @@
             full(3, HALF, 128),
             full(16, HALF),
             full(16, HALF),
-            low(4, 2, 2, 2, SUB, COLS),
+            full(16, HALF),
+            full(16, HALF),
+            low(SLOTS, 2, 2, 2, SUB, COLS),
             low(CHUNKS, 2, 2, SUB, COLS),
             low(CHUNKS, 2, SUB, COLS),
             low(CHUNKS, SUB, COLS),
@@ -798,15 +797,15 @@
             full(2, 16, COLS),
             full(2, 16, COLS),
             full(4, 16, COLS),
-            dma((12,)),
+            dma((10,)),
             dma((2,)),
             dma((2,)),
             dma((7, CHUNKS)),
             dma((7, CHUNKS)),
             dma((5,)),
             dma((5,)),
-            dma((2,)),
-            dma((2,)),
+            dma((14,)),
+            dma((14,)),
             dma((CHUNKS,)),
             dma((2,)),
         ],
@@ -879,45 +878,29 @@
     width = 768
     patch = patches[0]
     cot = cotangent[0]
-    patch_x = lax.ppermute(patch, "tm", swap)
+    y = lax.axis_index("tm")
     ids = segment_ids[0]
-    ids_x = lax.ppermute(ids, "tm", swap)
-    table = jnp.concatenate(
-        [
-            jnp.stack(
-                [
-                    mask_embed,
-                    norm1_gain,
-                    norm1_bias,
-                    query_bias,
-                    value_bias,
-                    out_bias,
-                    norm2_gain,
-                    norm2_bias,
-                    down_bias,
-                ]
-            ),
-            up_bias.reshape(4, 768),
-            jnp.zeros((3, 768), BF16),
-        ]
-    ).astype(F32)
+    ids_row = lax.pad(ids.astype(BF16)[None], jnp.zeros((), BF16), ((0, 15, 0), (0, width - HALF, 0)))
+    near = jnp.concatenate([lax.dynamic_slice(patch, ((1 - y) * TILE, 0), (TILE, width)), ids_row])
+    near_x = lax.ppermute(near, "tm", swap)
+    far_x = lax.ppermute(lax.dynamic_slice(patch, (y * TILE, 0), (TILE, width)), "tm", swap)
+    ids_x = near_x[TILE, :HALF].astype(jnp.int32)
+    table = tabulate(
+        (mask_embed, norm1_gain, norm1_bias, query_bias, value_bias, out_bias, norm2_gain, norm2_bias, down_bias)
+    )
     lane = jnp.arange(128)[None, :]
     qa = jnp.where(ids[:, None] == lane, 1.0, 0.0).astype(BF16)
     ka = jnp.where((lane >= 6) | (ids[:, None] == lane), 0.0, neg_large).astype(BF16)
     qxa = jnp.where(ids_x[:, None] == lane, 1.0, 0.0).astype(BF16)
     kxa = jnp.where((lane >= 6) | (ids_x[:, None] == lane), 0.0, neg_large).astype(BF16)
-    hidden1, qkv = front(False, patch, mask_positions, table, w_qkv)
-    unused, qkv_x = front(True, patch_x, mask_positions, table, w_qkv)
-    attended, lse = attend(qkv, qkv_x, qa, ka, kxa)
-    lse_rows = lse[:, :16].T
-    lse_rows_x = lax.ppermute(lse_rows, "tm", swap)
-    middle, hidden2, activated, grad_upper, up_sums = middle_part(
-        patch, mask_positions, table, attended, w_out, cot, w_up, w_down, up_bias.astype(F32)[None]
-    )
+    qkv, hidden1 = front(own_kernel, patch, mask_positions, table, w_qkv)
+    (other_near,) = front(partial(other_kernel, True), near_x, mask_positions, table, w_qkv)
+    (other_far,) = front(partial(other_kernel, False), far_x, mask_positions, table, w_qkv)
+    attended_near, attended_far, lse_near, lse_far = attend(qkv, other_near, other_far, qa, ka, kxa)
     parts, output, grad_patches, v = backward(
-        (activated, cot, grad_upper, middle, hidden2, w_out, qkv, qkv_x, attended, hidden1, patch, w_qkv),
+        (cot, w_out, qkv, hidden1, patch, w_qkv, other_near, other_far, attended_near, attended_far),
         (w_up, w_down),
-        (qa, ka, qxa, kxa, lse_rows, lse_rows_x, table, mask_positions, up_sums),
+        (qa, ka, qxa, kxa, lse_near, lse_far, table, mask_positions, up_bias.astype(F32)[None]),
     )
     grad_down, grad_up, grad_out, grad_qkv = widen(parts)
     return (

time: 223 us -> 201 us (0.901)
  Pallas kernels: 196 us -> 184 us
  local copies, waits for them, and re-layouts: 14.2 us -> 6.65 us
    pallas_call x3 -> x4, Pallas kernels: 30 us -> 17.9 us  [the longest x3 16.5 us: front(): pl.pallas_call(kernel, grid=(length // TILE,), out_shape=tuple((jax.Shape...]
    another operation x9 -> x0, local copies, waits for them, and re-layouts: 6.16 us -> none  [block_shards(): jnp.stack([mask_embed, norm1_gain, norm1_bias, query_bias, value_bias, ou...]
    ppermute x3 -> x2, starting transfers between devices: 4.94 us -> 3.14 us  [the longest x1 3.06 us: block_shards(): lax.ppermute(lax.dynamic_slice(patch, (y * TILE, 0), (TILE, width)), 'tm'...]
  transfers between devices with their start and end apart: 3 -> 2, of which waited for: 1 -> 1; matrix products, arithmetic and copies ran while one was open for 4% -> 1% of each run, Pallas kernels for 10% -> 7%
where the time goes in v1:
time: 201 us; the launch traced here: 200 us
  Pallas kernels  184 us (92%)
  local copies, waits for them, and re-layouts  6.65 us (3%)
  starting transfers between devices  3.14 us (2%)
  other arithmetic  3.04 us (2%)
  waiting for transfers between devices  2.17 us (1%)
    pallas_call x1, Pallas kernels, backward(): pl.pallas_call(halves_kernel, out_shape=(jax.ShapeDtypeStruct((CHUNKS, 2,...  140 us
    pallas_call x3, Pallas kernels, front(): pl.pallas_call(kernel, grid=(length // TILE,), out_shape=tuple((jax.Shape...  16.5 us
    pallas_call x1, Pallas kernels, attend(): pl.pallas_call(attend_kernel, grid=(6,), out_shape=(jax.ShapeDtypeStruct(...  14.3 us
    pallas_call x1, Pallas kernels, widen(): pl.pallas_call(widen_kernel, grid=(12,), out_shape=(jax.ShapeDtypeStruct(...  12.1 us
  transfers between devices with their start and end apart: 2, of which 1 were waited for; matrix products, arithmetic and copies ran while one was open for 1% of the time, Pallas kernels for 7%

profile of v1, /device:TPU:0, one launch (start us, length us, event | category | flops | bytes accessed | tf_op | source)
XLA Modules:
  0.0 200.0 jit_solution(5272708288510850520)
XLA Ops:
  0.6 1.2 dynamic-slice_bitcast_fusion
  1.8 3.1 %collective-permute-start.1 = (bf16[256,768]{1,0:T(8,128)(2,1)S(1)}, bf16[256,768]{1,0:T(8,128)(2,1)S(1)}, u32[]{:S(2)}, u32[]{:S(2)}) collective-permute-start(bf16[256,768]{1,0:T(8,128)(2,1)S(1)} %get-tuple-element.53), channel_id=1, source_target_pairs={{0,1},{1,0},{2,3},{3,2},{4,5},{5,4},{6,7},{7,6},{8,9},{9,8},{10,11... | collective-permute-start | bytes 1179656 | tf_op jit(solution)/shard_map/ppermute | solution.py:886
  4.9 0.7 convert_element_type.27
  5.6 0.1 collective-permute-start
  5.7 1.3 broadcast_in_dim.38
  7.0 1.5 shard_map.297.table_ref
  8.4 6.7 %shard_map.298 = (bf16[512,2304]{1,0:T(8,128)(2,1)}, bf16[512,768]{1,0:T(8,128)(2,1)}) custom-call(bf16[512,768]{1,0:T(8,128)(2,1)} %bitcast.14, s32[1,409]{1,0:T(1,128)} %marks_ref.7, f32[16,768]{1,0:T(8,128)} %shard_map.297.table_ref, bf16[768,2304]{1,0:T(8,128)(2,1)} %wq_h.1), custom_call_target="tpu_custom_call" | custom-call | flops 1811939328 | bytes 8388608 | tf_op jit(solution)/shard_map/pallas_call | solution.py:203
  15.1 0.0 collective-permute-done.1.p_ref
  15.1 0.0 copy-start.3
  15.2 0.7 copy-done.3
  15.9 4.9 %shard_map.300.kf_ref.vf_ref.otf_h = bf16[256,2304]{1,0:T(8,128)(2,1)} custom-call(bf16[256,768]{1,0:T(8,128)(2,1)} %copy-done.3, s32[1,409]{1,0:T(1,128)} %marks_ref.7, f32[16,768]{1,0:T(8,128)} %shard_map.297.table_ref, bf16[768,2304]{1,0:T(8,128)(2,1)} %wq_h.1), custom_call_target="tpu_custom_call" | custom-call | flops 905969664 | bytes 8388608 | tf_op jit(solution)/shard_map/pallas_call | solution.py:203
  20.8 2.2 %collective-permute-done.p_ref = bf16[272,768]{1,0:T(8,128)(2,1)S(1)} collective-permute-done((bf16[272,768]{1,0:T(8,128)(2,1)S(1)}, bf16[272,768]{1,0:T(8,128)(2,1)S(1)}, u32[]{:S(2)}, u32[]{:S(2)}) %collective-permute-start) | collective-permute-done | bytes 417824 | tf_op jit(solution)/shard_map/ppermute | solution.py:885
  23.0 0.0 copy-done.4
  23.0 1.0 select_convert_fusion
  24.0 0.0 copy-done.2
  24.0 4.9 %shard_map.299.kn_ref.vn_ref.otn_h = bf16[256,2304]{1,0:T(8,128)(2,1)} custom-call(bf16[272,768]{1,0:T(8,128)(2,1)} %copy-done.2, s32[1,409]{1,0:T(1,128)} %marks_ref.7, f32[16,768]{1,0:T(8,128)} %shard_map.297.table_ref, bf16[768,2304]{1,0:T(8,128)(2,1)} %wq_h.1), custom_call_target="tpu_custom_call" | custom-call | flops 905969664 | bytes 8388608 | tf_op jit(solution)/shard_map/pallas_call | solution.py:203
  28.9 14.3 %shard_map.301 = (bf16[256,768]{1,0:T(8,128)(2,1)}, bf16[256,768]{1,0:T(8,128)(2,1)}, f32[16,256]{1,0:T(8,128)}, f32[16,256]{1,0:T(8,128)}) custom-call(bf16[512,2304]{1,0:T(8,128)(2,1)} %get-tuple-element.30.q_ref.k_ref.v_ref.qkv_h, bf16[512,2304]{1,0:T(8,128)(2,1)} %get-tuple-element.30.q_ref.k_ref.v_ref.qkv_h, ...), custom_call_target="tpu_custom_call" | custom-call | flops 1610612736 | bytes 8388608 | tf_op jit(solution)/shard_map/pallas_call | solution.py:271
  43.2 140.0 %shard_map.302 = (bf16[24,2,2,96,384]{4,3,2,1,0:T(8,128)(2,1)}, bf16[512,768]{1,0:T(8,128)(2,1)}, bf16[512,768]{1,0:T(8,128)(2,1)}, f32[16,384]{1,0:T(8,128)}) custom-call(bf16[512,768]{1,0:T(8,128)(2,1)} %bitcast.18, bf16[768,768]{1,0:T(8,128)(2,1)} %wo_h.1, bf16[512,2304]{1,0:T(8,128)(2,1)} %get-tuple-element.30.q_ref.k_ref.v_ref.qkv_h, ...), custom_call_target="tpu_custom_call" | custom-call | tf_op jit(solution)/shard_map/pallas_call | solution.py:760
  183.2 1.7 slice_reduce_fusion
  184.9 0.7 slice.42
  185.6 12.1 %shard_map.303 = (f32[1536,768]{1,0:T(8,128)}, f32[384,3072]{1,0:T(8,128)}, f32[384,768]{1,0:T(8,128)}, f32[384,2304]{1,0:T(8,128)}) custom-call(bf16[24,384,384]{2,1,0:T(8,128)(2,1)} %bitcast.12, bf16[24,384,384]{2,1,0:T(8,128)(2,1)} %bitcast.13), custom_call_target="tpu_custom_call" | custom-call | tf_op jit(solution)/shard_map/pallas_call | solution.py:835
  197.7 0.6 reshape.54
  198.3 0.9 copy.36
  199.1 0.9 copy.37
  (9 shorter events, 0.1 us)
Async XLA Ops:
  1.8 13.3 %collective-permute-start.1 = (bf16[256,768]{1,0:T(8,128)(2,1)S(1)}, bf16[256,768]{1,0:T(8,128)(2,1)S(1)}, u32[]{:S(2)}, u32[]{:S(2)}) collective-permute-start(bf16[256,768]{1,0:T(8,128)(2,1)S(1)} %get-tuple-element.53), channel_id=1, source_target_pairs={{0,1},{1,0},{2,3},{3,2},{4,5},{5,4},{6,7},{7,6},{8,9},{9,8},{10,11... | collective-permute-start | bytes 1179656 | tf_op jit(solution)/shard_map/ppermute | solution.py:886
  5.6 17.3 %collective-permute-start = (bf16[272,768]{1,0:T(8,128)(2,1)S(1)}, bf16[272,768]{1,0:T(8,128)(2,1)S(1)}, u32[]{:S(2)}, u32[]{:S(2)}) collective-permute-start(bf16[272,768]{1,0:T(8,128)(2,1)S(1)} %fusion.1), channel_id=1, source_target_pairs={{0,1},{1,0},{2,3},{3,2},{4,5},{5,4},{6,7},{7,6},{8,9},{9,8},{10,11... | collective-permute-start | bytes 1253384 | tf_op jit(solution)/shard_map/ppermute | solution.py:885
  15.1 7.8 %copy-start.4 = (s32[1,512]{1,0:T(1,128)S(1)}, s32[1,512]{1,0:T(1,128)}, u32[]{:S(2)}) copy-start(s32[1,512]{1,0:T(1,128)} %param.19) | copy-start | bytes 6148
  15.1 0.7 copy-start.3
  23.0 1.0 copy-start.2
  185.6 12.7 %copy-start.1 = (bf16[512,768]{1,0:T(8,128)(2,1)S(1)}, bf16[512,768]{1,0:T(8,128)(2,1)}, u32[]{:S(2)}) copy-start(bf16[512,768]{1,0:T(8,128)(2,1)} %get-tuple-element.36) | copy-start | bytes 2359300
  185.6 13.6 %copy-start = (bf16[512,768]{1,0:T(8,128)(2,1)S(1)}, bf16[512,768]{1,0:T(8,128)(2,1)}, u32[]{:S(2)}) copy-start(bf16[512,768]{1,0:T(8,128)(2,1)} %get-tuple-element.37) | copy-start | bytes 2359300

commit v2 on v1

--- a/solution.py
+++ b/solution.py
@@ -88,7 +88,7 @@
 MESH = pl.DeviceIdType.MESH
 SUB = 96
 COLS = 384
-LAGS = (0, 1, 5, 6, 7, 9, 11, 12)
+LAGS = (0, 1, 4, 5, 6, 8, 9, 10)
 
 
 def places():
@@ -140,23 +140,6 @@
     return lax.dot_general(a, b, (((0,), (0,)), ((), ())), preferred_element_type=F32)
 
 
-def table_kernel(*refs):
-    table_ref = refs[-1]
-    table_ref[...] = jnp.zeros_like(table_ref)
-    for i, ref in enumerate(refs[:-1]):
-        table_ref[i : i + 1, :] = ref[...].astype(F32).reshape(1, 768)
-
-
-def tabulate(smalls):
-    near = pl.BlockSpec(memory_space=pltpu.VMEM)
-    return pl.pallas_call(
-        table_kernel,
-        out_shape=jax.ShapeDtypeStruct((16, 768), F32),
-        in_specs=[near] * len(smalls),
-        out_specs=near,
-    )(*smalls)
-
-
 def standard(values):
     center = values - jnp.mean(values, axis=-1, keepdims=True)
     scale_inv = lax.rsqrt(jnp.mean(center * center, axis=-1, keepdims=True) + norm_eps)
@@ -169,7 +152,7 @@
     return flagged, jnp.where(flagged, embed, patch.astype(F32))
 
 
-def project_tile(patch, first, marks_ref, table_ref, w_ref, qkv_ref):
+def project_tile(patch, first, marks_ref, table_ref, w_ref, qkv_ref, rows):
     unused, inputs = masked_inputs(patch, first, marks_ref[...], table_ref[R_EMBED : R_EMBED + 1, :])
     normed, unused = standard(inputs)
     hidden = (normed * table_ref[R_G1 : R_G1 + 1, :] + table_ref[R_B1 : R_B1 + 1, :]).astype(BF16)
@@ -181,106 +164,171 @@
             project = (project + table_ref[R_QB : R_QB + 1, bias]) * QUERY_SCALE
         elif part >= 4:
             project = project + table_ref[R_VB : R_VB + 1, bias]
-        qkv_ref[:, cols] = project.astype(BF16)
+        qkv_ref[rows, cols] = project.astype(BF16)
     return hidden
 
 
-def own_kernel(p_ref, marks_ref, table_ref, w_ref, qkv_ref, h1_ref):
-    first = lax.axis_index("tm") * HALF + pl.program_id(0) * TILE
-    h1_ref[...] = project_tile(p_ref[...], first, marks_ref, table_ref, w_ref, qkv_ref)
-
-
-def other_kernel(near, p_ref, marks_ref, table_ref, w_ref, qkv_ref):
-    y = lax.axis_index("tm")
-    first = (1 - y) * HALF + (y if near else 1 - y) * TILE
-    project_tile(p_ref[...], first, marks_ref, table_ref, w_ref, qkv_ref)
-
-
-def front(kernel, patch, marks, table, w_qkv):
-    own = patch.shape[0] == HALF
-    length = HALF if own else TILE
-    widths = (2304, 768) if own else (2304,)
-    return pl.pallas_call(
-        kernel,
-        grid=(length // TILE,),
-        out_shape=tuple(jax.ShapeDtypeStruct((length, n), BF16) for n in widths),
-        in_specs=[
-            pl.BlockSpec((TILE, 768), lambda i: (i, 0)),
-            pl.BlockSpec(marks.shape, lambda i: (0, 0)),
-            pl.BlockSpec(table.shape, lambda i: (0, 0)),
-            pl.BlockSpec((768, 2304), lambda i: (0, 0), pipeline_mode=pl.Buffered(1)),
-        ],
-        out_specs=tuple(pl.BlockSpec((TILE, n), lambda i: (i, 0)) for n in widths),
-        cost_estimate=pl.CostEstimate(flops=2 * length * 768 * 2304, bytes_accessed=8 << 20, transcendentals=0),
-    )(patch, marks, table, w_qkv)
-
-
-def attend_kernel(
-    q_ref, k_ref, v_ref, kn_ref, vn_ref, kf_ref, vf_ref, qa_ref, ka_ref, kxa_ref, on_ref, of_ref, ln_ref, lf_ref, marks_ref
+def first_kernel(
+    patch_h, wq_h, ids_ref, marks_ref, s0, s1, s2, s3, s4, s5, s6, s7, s8,
+    qkv_h, h1_h, qkvx_h, att_h, lse_ref, qa_ref, ka_ref, qxa_ref, kxa_ref, table_ref,
+    patch, patch_x, ids_x, wq, qkv, qkvx, h1, att, acc, tops, sums, insem, ssem, rsem, outsem,
 ):
-    y = lax.axis_index("tm")
-    pair = pl.program_id(0)
+    core, x, y, peers = places()
+    partner = peers[1]
     lane = lax.broadcasted_iota(jnp.int32, (1, 128), 1)
 
     def rows_of(index):
         return pl.ds(pl.multiple_of(index * TILE, TILE), TILE)
 
-    blocks = [
-        (k_ref, ka_ref[...], v_ref),
-        (kn_ref, kxa_ref[rows_of(y), :], vn_ref),
-        (kf_ref, kxa_ref[rows_of(1 - y), :], vf_ref),
+    def lanes(start):
+        return pl.ds(pl.multiple_of(start, 128), 128)
+
+    near, far = rows_of(1 - y), rows_of(y)
+    loads = [pltpu.make_async_copy(a, b, insem.at[i]) for i, (a, b) in enumerate(((patch_h, patch), (wq_h, wq)))]
+    for load in loads:
+        load.start()
+    greet((partner,))
+    loads[0].wait()
+    sends = [
+        pltpu.make_async_remote_copy(
+            src_ref=src, dst_ref=dst, send_sem=ssem.at[i], recv_sem=rsem.at[i], device_id=partner, device_id_type=MESH
+        )
+        for i, (src, dst) in enumerate(
+            (
+                (ids_ref, ids_x),
+                (patch.at[near, :], patch_x.at[near, :]),
+                (patch.at[far, :], patch_x.at[far, :]),
+            )
+        )
     ]
-    all_keys = [jnp.concatenate([k[...], a], axis=1) for k, a, unused in blocks]
-    for far, number, o_ref, lse_ref in ((0, 3, on_ref, ln_ref), (1, 2, of_ref, lf_ref)):
-        rows = rows_of(y if far else 1 - y)
-        q = q_ref[rows, :]
-        qa = qa_ref[rows, :]
-        kept = None
-        marks = jnp.where(pair == 0, 0.0, marks_ref[far])
-        for h in range(2):
-            mine = (lane // 64) == h
-            query = jnp.concatenate([jnp.where(mine, q, 0), qa], axis=1)
-            scores = [dot_t(query, key) for key in all_keys[:number]]
-            peak = jnp.max(scores[0], axis=-1, keepdims=True)
-            for more in scores[1:]:
-                peak = jnp.maximum(peak, jnp.max(more, axis=-1, keepdims=True))
-            total = 0.0
-            out = 0.0
-            for score, block in zip(scores, blocks):
-                weights = jnp.exp(score - peak)
-                total = total + jnp.sum(weights, axis=-1, keepdims=True)
-                out = out + dot(weights.astype(BF16), block[2][...])
-            out = out / total
-            kept = out if h == 0 else jnp.where(mine, out, kept)
-            marks = jnp.where(lane == 2 * pair + h, peak + jnp.log(total), marks)
-        o_ref[...] = kept.astype(BF16)
-        marks_ref[far] = marks
-
-    @pl.when(pair == 5)
-    def _():
-        ln_ref[...] = marks_ref[0].T[:16, :]
-        lf_ref[...] = marks_ref[1].T[:16, :]
-
-
-def attend(qkv, near, far, qa, ka, kxa):
-    def block(first, length):
-        return pl.BlockSpec((length, 128), lambda i: (0, first + i))
-
-    whole = pl.BlockSpec((HALF, 128), lambda i: (0, 0))
-    stat = pl.BlockSpec((16, TILE), lambda i: (0, 0))
+    for send in sends:
+        send.start()
+    table_ref[...] = jnp.zeros_like(table_ref)
+    for i, ref in enumerate((s0, s1, s2, s3, s4, s5, s6, s7, s8)):
+        table_ref[i : i + 1, :] = ref[...].astype(F32).reshape(1, 768)
+
+    def masks(ids, one_ref, mask_ref):
+        hot = jnp.where(lax.broadcasted_iota(jnp.int32, (128, HALF), 0) == ids, 1.0, 0.0).T
+        one_ref[...] = hot.astype(BF16)
+        mask_ref[...] = jnp.where((lane >= 6) | (hot > 0.5), 0.0, neg_large).astype(BF16)
+
+    masks(ids_ref[...], qa_ref, ka_ref)
+    loads[1].wait()
+
+    def own(i, carry):
+        rows = rows_of(i)
+        h1[rows, :] = project_tile(patch[rows, :], y * HALF + i * TILE, marks_ref, table_ref, wq, qkv, rows)
+        return carry
+
+    lax.fori_loop(0, 2, own, 0)
+    stores = [
+        pltpu.make_async_copy(a, b, outsem.at[i])
+        for i, (a, b) in enumerate(((qkv, qkv_h), (h1, h1_h), (qkvx, qkvx_h), (att, att_h)))
+    ]
+    stores[0].start()
+    stores[1].start()
+
+    def absorb(groups, source, places_of, mask, first):
+        def pair(p, carry):
+            keys = jnp.concatenate([source[places_of, lanes(768 + p * 128)], mask], axis=1)
+            values = source[places_of, lanes(1536 + p * 128)]
+            for rows in groups:
+                q = qkv[rows, lanes(p * 128)]
+                qa = qa_ref[rows, :]
+                top, total = tops[rows, :], sums[rows, :]
+                if first:
+                    top, total = jnp.where(p == 0, 0.0, top), jnp.where(p == 0, 0.0, total)
+                else:
+                    old = acc[rows, lanes(p * 128)]
+                new_top, new_total = top, total
+                kept = None
+                for h in range(2):
+                    mine = (lane // 64) == h
+                    here = lane == 2 * p + h
+                    scores = dot_t(jnp.concatenate([jnp.where(mine, q, 0), qa], axis=1), keys)
+                    peak = jnp.max(scores, axis=-1, keepdims=True)
+                    if not first:
+                        before = jnp.sum(jnp.where(here, top, 0.0), axis=-1, keepdims=True)
+                        peak = jnp.maximum(before, peak)
+                        scale = jnp.exp(before - peak)
+                    weights = jnp.exp(scores - peak)
+                    number = jnp.sum(weights, axis=-1, keepdims=True)
+                    out = dot(weights.astype(BF16), values)
+                    if not first:
+                        number = number + scale * jnp.sum(jnp.where(here, total, 0.0), axis=-1, keepdims=True)
+                        out = out + scale * old
+                    kept = out if h == 0 else jnp.where(mine, out, kept)
+                    new_top = jnp.where(here, peak, new_top)
+                    new_total = jnp.where(here, number, new_total)
+                acc[rows, lanes(p * 128)] = kept
+                tops[rows, :] = new_top
+                sums[rows, :] = new_total
+            return carry
+
+        lax.fori_loop(0, 6, pair, 0)
+
+    both = (slice(0, TILE), slice(TILE, HALF))
+    absorb(both, qkv, slice(None), ka_ref[...], True)
+    sends[0].wait_recv()
+    masks(ids_x[...], qxa_ref, kxa_ref)
+    sends[1].wait_recv()
+    project_tile(patch_x[far, :], (1 - y) * HALF + y * TILE, marks_ref, table_ref, wq, qkvx, far)
+
+    absorb(both, qkvx, far, kxa_ref[far, :], False)
+    sends[2].wait_recv()
+    project_tile(patch_x[near, :], (1 - y) * HALF + (1 - y) * TILE, marks_ref, table_ref, wq, qkvx, near)
+    stores[2].start()
+    absorb((near,), qkvx, near, kxa_ref[near, :], False)
+    total = jnp.where(lane < 12, sums[...], 1.0)
+    lse_ref[...] = (tops[...] + jnp.log(total)).T[:16, :]
+    for p in range(6):
+        for i in range(2):
+            rows = slice(i * TILE, i * TILE + TILE)
+            low, high = sums[rows, 2 * p : 2 * p + 1], sums[rows, 2 * p + 1 : 2 * p + 2]
+            cols = slice(p * 128, p * 128 + 128)
+            att[rows, cols] = (acc[rows, cols] / jnp.where(lane < 64, low, high)).astype(BF16)
+    stores[3].start()
+    for send in sends:
+        send.wait_send()
+    for store in stores:
+        store.wait()
+
+
+def first_half(patch, w_qkv, ids, marks, smalls):
+    hbm = pl.BlockSpec(memory_space=pl.ANY)
+    near = pl.BlockSpec(memory_space=pltpu.VMEM)
+    dma = pltpu.SemaphoreType.DMA
+
+    def low(*shape):
+        return pltpu.VMEM(shape, BF16)
+
     return pl.pallas_call(
-        attend_kernel,
-        grid=(6,),
-        out_shape=(jax.ShapeDtypeStruct((TILE, 768), BF16),) * 2 + (jax.ShapeDtypeStruct((16, TILE), F32),) * 2,
-        in_specs=[block(0, HALF), block(6, HALF), block(12, HALF)]
-        + [block(6, TILE), block(12, TILE)] * 2
-        + [whole] * 3,
-        out_specs=(block(0, TILE), block(0, TILE), stat, stat),
-        scratch_shapes=[pltpu.VMEM((2, TILE, 128), F32)],
-        cost_estimate=pl.CostEstimate(
-            flops=4 * 12 * HALF * 1024 * 64, bytes_accessed=8 << 20, transcendentals=12 * HALF * 1024
-        ),
-    )(qkv, qkv, qkv, near, near, far, far, qa, ka, kxa)
+        first_kernel,
+        out_shape=tuple(jax.ShapeDtypeStruct((HALF, n), BF16) for n in (2304, 768, 2304, 768))
+        + (jax.ShapeDtypeStruct((16, HALF), F32),)
+        + (jax.ShapeDtypeStruct((HALF, 128), BF16),) * 4
+        + (jax.ShapeDtypeStruct((16, 768), F32),),
+        in_specs=[hbm, hbm] + [near] * (2 + len(smalls)),
+        out_specs=(hbm,) * 4 + (near,) * 6,
+        scratch_shapes=[
+            low(HALF, 768),
+            low(HALF, 768),
+            pltpu.VMEM((1, HALF), jnp.int32),
+            low(768, 2304),
+            low(HALF, 2304),
+            low(HALF, 2304),
+            low(HALF, 768),
+            low(HALF, 768),
+            pltpu.VMEM((HALF, 768), F32),
+            pltpu.VMEM((HALF, 128), F32),
+            pltpu.VMEM((HALF, 128), F32),
+            dma((2,)),
+            dma((3,)),
+            dma((3,)),
+            dma((4,)),
+        ],
+        compiler_params=pltpu.CompilerParams(collective_id=1, has_side_effects=True, vmem_limit_bytes=67043328),
+    )(patch, w_qkv, ids, marks, *smalls)
 
 
 ERFC_P = 0.3275911
@@ -323,25 +371,22 @@
 
 
 def halves_kernel(
-    cot_h, wo_h, qkv_h, h1_h, patch_h, wq_h, otn_h, otf_h, atn_h, atf_h, wu_h, wd_h,
-    qa_ref, ka_ref, qxa_ref, kxa_ref, lsen_ref, lsef_ref, table_ref, marks_ref, ub_ref,
+    cot_h, wo_h, qkv_h, h1_h, patch_h, wq_h, qkvx_h, att_h, wu_h, wd_h,
+    qa_ref, ka_ref, qxa_ref, kxa_ref, lse_ref, table_ref, marks_ref, ub_ref,
     parts_h, out_h, gp_h, vec_out,
     cot, wo, qkv, h1, patch, wq, qkvx, att, wu, wd,
-    act, gu, mid, h2, acc, gb, do, dox, dqkv, dq, dk, dv, drow, dxrow, lse_ref, lsex_ref,
+    act, gu, mid, h2, acc, gb, do, dox, dqkv, dq, dk, dv, drow, dxrow, lsex_ref,
     g, r1, r2, r3, r4, r5, done, v0, v1, v2,
     insem, wusem, wdsem, ssem, rsem, vs, vr, xs, xr, outsem, lastsem,
 ):
     core, x, y, peers = places()
     pair, yp, xp, zp1, zp2 = peers
     lane = lax.broadcasted_iota(jnp.int32, (1, 128), 1)
-    near_rows = pl.ds(pl.multiple_of((1 - y) * TILE, TILE), TILE)
-    far_rows = pl.ds(pl.multiple_of(y * TILE, TILE), TILE)
     inputs = (
         (cot_h, cot), (wo_h, wo), (qkv_h, qkv), (h1_h, h1), (patch_h, patch), (wq_h, wq),
-        (otn_h, qkvx.at[far_rows, :]), (otf_h, qkvx.at[near_rows, :]),
-        (atn_h, att.at[near_rows, :]), (atf_h, att.at[far_rows, :]),
-    )
-    COT, WO, QKV, H1, PATCH, WQ, OTN, OTF, ATN, ATF = range(10)
+        (qkvx_h, qkvx), (att_h, att),
+    )
+    COT, WO, QKV, H1, PATCH, WQ, QKVX, ATT = range(8)
 
     def lanes(start, size=128):
         return pl.ds(pl.multiple_of(start, 128), size)
@@ -359,12 +404,12 @@
         rows = pl.ds(pl.multiple_of(part_of(n) * FF_TILE, FF_TILE), FF_TILE)
         return pltpu.make_async_copy(wd_h.at[rows, :], wd.at[n % 2], wdsem.at[n % 2])
 
-    for i in (PATCH, WO, ATN, ATF):
+    for i in (PATCH, WO, ATT):
         load(i).start()
     for n in range(2):
         up_tile(n).start()
         down_tile(n).start()
-    for i in (COT, QKV, OTN, OTF, H1, WQ):
+    for i in (COT, QKV, QKVX, H1, WQ):
         load(i).start()
     greet(peers)
 
@@ -634,12 +679,10 @@
         lax.fori_loop(0, 4, tile, 0)
         pltpu.make_async_copy(att, gp_h, lastsem.at[1]).start()
 
-    lse_ref[:, near_rows] = lsen_ref[...]
-    lse_ref[:, far_rows] = lsef_ref[...]
     far_copy(0).start()
     acc[...] = jnp.zeros_like(acc)
     v0[...] = jnp.zeros_like(v0)
-    for i in (PATCH, WO, ATN, ATF):
+    for i in (PATCH, WO, ATT):
         load(i).wait()
     enter()
     load(COT).wait()
@@ -661,7 +704,7 @@
                 for i in names:
                     load(i).wait()
 
-        need(2, QKV, OTN, OTF, H1, WQ)
+        need(2, QKV, QKVX, H1, WQ)
         run(T_FORWARD, forward)
         run(
             EMIT_DOWN,
@@ -756,7 +799,7 @@
         return pltpu.VMEM(shape, F32)
 
     dma = pltpu.SemaphoreType.DMA
-    held = [pltpu.VMEM(a.shape, a.dtype) for a in big[:6]] + [low(HALF, 2304), low(HALF, 768)]
+    held = [pltpu.VMEM(a.shape, a.dtype) for a in big]
     return pl.pallas_call(
         halves_kernel,
         out_shape=(
@@ -786,7 +829,6 @@
             full(16, HALF),
             full(16, HALF),
             full(16, HALF),
-            full(16, HALF),
             low(SLOTS, 2, 2, 2, SUB, COLS),
             low(CHUNKS, 2, 2, SUB, COLS),
             low(CHUNKS, 2, SUB, COLS),
@@ -797,7 +839,7 @@
             full(2, 16, COLS),
             full(2, 16, COLS),
             full(4, 16, COLS),
-            dma((10,)),
+            dma((8,)),
             dma((2,)),
             dma((2,)),
             dma((7, CHUNKS)),
@@ -874,33 +916,19 @@
     down_bias,
     cotangent,
 ):
-    swap = [(0, 1), (1, 0)]
-    width = 768
     patch = patches[0]
     cot = cotangent[0]
-    y = lax.axis_index("tm")
-    ids = segment_ids[0]
-    ids_row = lax.pad(ids.astype(BF16)[None], jnp.zeros((), BF16), ((0, 15, 0), (0, width - HALF, 0)))
-    near = jnp.concatenate([lax.dynamic_slice(patch, ((1 - y) * TILE, 0), (TILE, width)), ids_row])
-    near_x = lax.ppermute(near, "tm", swap)
-    far_x = lax.ppermute(lax.dynamic_slice(patch, (y * TILE, 0), (TILE, width)), "tm", swap)
-    ids_x = near_x[TILE, :HALF].astype(jnp.int32)
-    table = tabulate(
-        (mask_embed, norm1_gain, norm1_bias, query_bias, value_bias, out_bias, norm2_gain, norm2_bias, down_bias)
-    )
-    lane = jnp.arange(128)[None, :]
-    qa = jnp.where(ids[:, None] == lane, 1.0, 0.0).astype(BF16)
-    ka = jnp.where((lane >= 6) | (ids[:, None] == lane), 0.0, neg_large).astype(BF16)
-    qxa = jnp.where(ids_x[:, None] == lane, 1.0, 0.0).astype(BF16)
-    kxa = jnp.where((lane >= 6) | (ids_x[:, None] == lane), 0.0, neg_large).astype(BF16)
-    qkv, hidden1 = front(own_kernel, patch, mask_positions, table, w_qkv)
-    (other_near,) = front(partial(other_kernel, True), near_x, mask_positions, table, w_qkv)
-    (other_far,) = front(partial(other_kernel, False), far_x, mask_positions, table, w_qkv)
-    attended_near, attended_far, lse_near, lse_far = attend(qkv, other_near, other_far, qa, ka, kxa)
+    qkv, hidden1, qkv_x, attended, lse, qa, ka, qxa, kxa, table = first_half(
+        patch,
+        w_qkv,
+        segment_ids,
+        mask_positions,
+        (mask_embed, norm1_gain, norm1_bias, query_bias, value_bias, out_bias, norm2_gain, norm2_bias, down_bias),
+    )
     parts, output, grad_patches, v = backward(
-        (cot, w_out, qkv, hidden1, patch, w_qkv, other_near, other_far, attended_near, attended_far),
+        (cot, w_out, qkv, hidden1, patch, w_qkv, qkv_x, attended),
         (w_up, w_down),
-        (qa, ka, qxa, kxa, lse_near, lse_far, table, mask_positions, up_bias.astype(F32)[None]),
+        (qa, ka, qxa, kxa, lse, table, mask_positions, up_bias.astype(F32)[None]),
     )
     grad_down, grad_up, grad_out, grad_qkv = widen(parts)
     return (

time: 201 us -> 191 us (0.950)
  local copies, waits for them, and re-layouts: 6.65 us -> 3.02 us
  starting transfers between devices: 3.14 us -> 0 us
  waiting for transfers between devices: 2.17 us -> 0 us
    ppermute x2 -> x0, starting transfers between devices: 3.14 us -> none  [the longest x1 3.06 us: block_shards(): lax.ppermute(lax.dynamic_slice(patch, (y * TILE, 0), (TILE, width)), 'tm'...]
    ppermute x2 -> x0, waiting for transfers between devices: 2.17 us -> none  [the longest x1 2.17 us: block_shards(): near_x = lax.ppermute(near, 'tm', swap)]
    pallas_call x5 -> x1, Pallas kernels: 32.2 us -> 32.6 us  [first_half(): pl.pallas_call(first_kernel, out_shape=tuple((jax.ShapeDtypeStruct((HALF,...]
  transfers between devices with their start and end apart: 2 -> 0, of which waited for: 1 -> 0; matrix products, arithmetic and copies ran while one was open for 1% -> 0% of each run, Pallas kernels for 7% -> 0%
where the time goes in v2:
time: 191 us
  Pallas kernels  186 us (97%)
  local copies, waits for them, and re-layouts  3.02 us (2%)
    pallas_call x1, Pallas kernels, backward(): pl.pallas_call(halves_kernel, out_shape=(jax.ShapeDtypeStruct((CHUNKS, 2,...  141 us
    pallas_call x1, Pallas kernels, first_half(): pl.pallas_call(first_kernel, out_shape=tuple((jax.ShapeDtypeStruct((HALF,...  32.6 us
    pallas_call x1, Pallas kernels, widen(): pl.pallas_call(widen_kernel, grid=(12,), out_shape=(jax.ShapeDtypeStruct(...  12.1 us

profile of v2, /device:TPU:0, one launch (start us, length us, event | category | flops | bytes accessed | tf_op | source)
XLA Modules:
  0.0 190.8 jit_solution(11924688601123242213)
XLA Ops:
  0.7 32.6 %shard_map.297 = (bf16[512,2304]{1,0:T(8,128)(2,1)}, bf16[512,768]{1,0:T(8,128)(2,1)}, bf16[512,2304]{1,0:T(8,128)(2,1)}, bf16[512,768]{1,0:T(8,128)(2,1)}, f32[...) custom-call(bf16[512,768]{1,0:T(8,128)(2,1)} %bitcast.8, ...), custom_call_target="tpu_custom_call" | custom-call | tf_op jit(solution)/shard_map/pallas_call | solution.py:305
  33.2 1.3 broadcast_in_dim.15
  34.5 141.1 %shard_map.298 = (bf16[24,2,2,96,384]{4,3,2,1,0:T(8,128)(2,1)}, bf16[512,768]{1,0:T(8,128)(2,1)}, bf16[512,768]{1,0:T(8,128)(2,1)}, f32[16,384]{1,0:T(8,128)}) custom-call(bf16[512,768]{1,0:T(8,128)(2,1)} %bitcast.12, bf16[768,768]{1,0:T(8,128)(2,1)} %wo_h.1, bf16[512,2304]{1,0:T(8,128)(2,1)} %get-tuple-element.34.qkv_h, ...), custom_call_target="tpu_custom_call" | custom-call | tf_op jit(solution)/shard_map/pallas_call | solution.py:803
  175.6 0.0 copy-start.2
  175.6 0.0 copy-start.1
  175.6 0.0 copy-start
  175.7 12.1 %shard_map.299 = (f32[1536,768]{1,0:T(8,128)}, f32[384,3072]{1,0:T(8,128)}, f32[384,768]{1,0:T(8,128)}, f32[384,2304]{1,0:T(8,128)}) custom-call(bf16[24,384,384]{2,1,0:T(8,128)(2,1)} %bitcast.6, bf16[24,384,384]{2,1,0:T(8,128)(2,1)} %bitcast.7), custom_call_target="tpu_custom_call" | custom-call | tf_op jit(solution)/shard_map/pallas_call | solution.py:877
  187.8 0.0 copy-done.2
  187.8 0.6 slice_reduce_fusion
  188.4 0.6 reshape.39
  189.0 0.0 copy-done.1
  189.0 0.9 copy.36
  189.9 0.0 copy-done
  189.9 0.9 copy.37
  (1 shorter events, 0.0 us)
Async XLA Ops:
  175.6 12.1 %copy-start.2 = (f32[16,384]{1,0:T(8,128)S(1)}, f32[16,384]{1,0:T(8,128)}, u32[]{:S(2)}) copy-start(f32[16,384]{1,0:T(8,128)} %get-tuple-element.46) | copy-start | bytes 73732
  175.6 13.4 %copy-start.1 = (bf16[512,768]{1,0:T(8,128)(2,1)S(1)}, bf16[512,768]{1,0:T(8,128)(2,1)}, u32[]{:S(2)}) copy-start(bf16[512,768]{1,0:T(8,128)(2,1)} %get-tuple-element.44) | copy-start | bytes 2359300
  175.6 14.2 %copy-start = (bf16[512,768]{1,0:T(8,128)(2,1)S(1)}, bf16[512,768]{1,0:T(8,128)(2,1)}, u32[]{:S(2)}) copy-start(bf16[512,768]{1,0:T(8,128)(2,1)} %get-tuple-element.45) | copy-start | bytes 2359300

commit v3 on v2

--- a/solution.py
+++ b/solution.py
@@ -375,7 +375,7 @@
     qa_ref, ka_ref, qxa_ref, kxa_ref, lse_ref, table_ref, marks_ref, ub_ref,
     parts_h, out_h, gp_h, vec_out,
     cot, wo, qkv, h1, patch, wq, qkvx, att, wu, wd,
-    act, gu, mid, h2, acc, gb, do, dox, dqkv, dq, dk, dv, drow, dxrow, lsex_ref,
+    act, gu, mid, h2, acc, gb, do, dox, dqkv, dq, dk, dv, drow, dxrow, lsex_ref, ub,
     g, r1, r2, r3, r4, r5, done, v0, v1, v2,
     insem, wusem, wdsem, ssem, rsem, vs, vr, xs, xr, outsem, lastsem,
 ):
@@ -524,7 +524,7 @@
         sums = jnp.zeros((1, FF_TILE), F32)
         for tile in range(HALF // TILE):
             rows = slice(tile * TILE, tile * TILE + TILE)
-            value, slope = gelu_and_slope(dot(h2[rows, :], wu[n % 2]) + ub_ref[:, cols])
+            value, slope = gelu_and_slope(dot(h2[rows, :], wu[n % 2]) + ub[:, cols])
             act[rows, cols] = value.astype(BF16)
             low = (dot_t(cot[rows, :], wd[n % 2]) * slope).astype(BF16)
             gu[rows, cols] = low
@@ -680,6 +680,7 @@
         pltpu.make_async_copy(att, gp_h, lastsem.at[1]).start()
 
     far_copy(0).start()
+    ub[...] = ub_ref[...].astype(F32).reshape(1, 3072)
     acc[...] = jnp.zeros_like(acc)
     v0[...] = jnp.zeros_like(v0)
     for i in (PATCH, WO, ATT):
@@ -703,6 +704,13 @@
             def _():
                 for i in names:
                     load(i).wait()
+
+        for s in range(2, 8):
+            c = t - LAGS[s]
+
+            @pl.when((c >= 0) & (c < CHUNKS))
+            def _():
+                stage(s, c)
 
         need(2, QKV, QKVX, H1, WQ)
         run(T_FORWARD, forward)
@@ -721,12 +729,14 @@
             emit(lambda half: h1[:, half * 384 : half * 384 + 384], right, 18 + p)
 
         run(EMIT_QKV, emit_qkv)
-        for s in range(2):
-            c = t - LAGS[s]
-
-            @pl.when((c >= 0) & (c < CHUNKS))
-            def _():
-                stage(s, c)
+        @pl.when(t < CHUNKS)
+        def _():
+            stage(0, t)
+
+        @pl.when((t >= LAGS[1]) & (t < CHUNKS + LAGS[1]))
+        def _():
+            stage(1, t - LAGS[1])
+
 
         run(T_SECOND, lambda n: second_norm())
         run(T_ATTENDED, lambda n: grad_attended())
@@ -747,13 +757,6 @@
 
         run(T_GRAD, grad_first)
         run(T_FIRST, lambda n: first_norm())
-
-        for s in range(2, 8):
-            c = t - LAGS[s]
-
-            @pl.when((c >= 0) & (c < CHUNKS))
-            def _():
-                stage(s, c)
 
         for s in range(6):
 
@@ -829,6 +832,7 @@
             full(16, HALF),
             full(16, HALF),
             full(16, HALF),
+            full(1, 3072),
             low(SLOTS, 2, 2, 2, SUB, COLS),
             low(CHUNKS, 2, 2, SUB, COLS),
             low(CHUNKS, 2, SUB, COLS),
@@ -857,16 +861,23 @@
     )(*big, *weights, *small)
 
 
-def widen_kernel(pair_ref, qkv_ref, down_ref, up_ref, out_ref, proj_ref):
+def widen_kernel(four_ref, qkv_ref, down_ref, up_ref, out_ref, proj_ref):
     i = pl.program_id(0)
-    for first, last, ref in ((0, 4, down_ref), (4, 8, up_ref), (8, 9, out_ref)):
+
+    @pl.when(i < 2)
+    def _():
+        for c in range(4):
+            rows = slice(c // 2 * 384, c // 2 * 384 + 384)
+            down_ref[rows, c % 2 * 384 : c % 2 * 384 + 384] = four_ref[c].astype(F32)
+
+    for first, last, ref in ((2, 4, up_ref), (4, 5, out_ref)):
 
         @pl.when((i >= first) & (i < last))
         def _():
-            for c in range(2):
-                ref[:, c * 384 : c * 384 + 384] = pair_ref[c].astype(F32)
-
-    @pl.when(i >= 9)
+            for c in range(ref.shape[1] // 384):
+                ref[:, c * 384 : c * 384 + 384] = four_ref[c].astype(F32)
+
+    @pl.when(i >= 5)
     def _():
         for p in range(6):
             proj_ref[:, p * 128 : p * 128 + 128] = qkv_ref[p].astype(F32)
@@ -876,7 +887,7 @@
     parts = parts.reshape(CHUNKS, 384, COLS)
     return pl.pallas_call(
         widen_kernel,
-        grid=(12,),
+        grid=(8,),
         out_shape=(
             jax.ShapeDtypeStruct((1536, 768), F32),
             jax.ShapeDtypeStruct((384, 3072), F32),
@@ -884,14 +895,14 @@
             jax.ShapeDtypeStruct((384, 2304), F32),
         ),
         in_specs=[
-            pl.BlockSpec((2, 384, COLS), lambda i: (jnp.minimum(i, 8), 0, 0)),
-            pl.BlockSpec((6, 384, 128), lambda i: (3, 0, jnp.maximum(i - 9, 0))),
+            pl.BlockSpec((4, 384, COLS), lambda i: (jnp.minimum(i, 4), 0, 0)),
+            pl.BlockSpec((6, 384, 128), lambda i: (3, 0, jnp.maximum(i - 5, 0))),
         ],
         out_specs=(
-            pl.BlockSpec((384, 768), lambda i: (jnp.minimum(i, 3), 0)),
-            pl.BlockSpec((384, 768), lambda i: (0, jnp.clip(i - 4, 0, 3))),
+            pl.BlockSpec((768, 768), lambda i: (jnp.minimum(i, 1), 0)),
+            pl.BlockSpec((384, 1536), lambda i: (0, jnp.clip(i - 2, 0, 1))),
             pl.BlockSpec((384, 768), lambda i: (0, 0)),
-            pl.BlockSpec((384, 768), lambda i: (0, jnp.maximum(i - 9, 0))),
+            pl.BlockSpec((384, 768), lambda i: (0, jnp.maximum(i - 5, 0))),
         ),
     )(parts, parts)
 
@@ -928,7 +939,7 @@
     parts, output, grad_patches, v = backward(
         (cot, w_out, qkv, hidden1, patch, w_qkv, qkv_x, attended),
         (w_up, w_down),
-        (qa, ka, qxa, kxa, lse, table, mask_positions, up_bias.astype(F32)[None]),
+        (qa, ka, qxa, kxa, lse, table, mask_positions, up_bias),
     )
     grad_down, grad_up, grad_out, grad_qkv = widen(parts)
     return (

time: 191 us -> 185 us (0.969)
  Pallas kernels: 186 us -> 181 us
    pallas_call x1, Pallas kernels: 141 us -> 138 us  [backward(): pl.pallas_call(halves_kernel, out_shape=(jax.ShapeDtypeStruct((CHUNKS, 2,...]
where the time goes in v3:
time: 185 us
  Pallas kernels  181 us (98%)
  local copies, waits for them, and re-layouts  3.02 us (2%)
    pallas_call x1, Pallas kernels, backward(): pl.pallas_call(halves_kernel, out_shape=(jax.ShapeDtypeStruct((CHUNKS, 2,...  138 us
    pallas_call x1, Pallas kernels, first_half(): pl.pallas_call(first_kernel, out_shape=tuple((jax.ShapeDtypeStruct((HALF,...  32.6 us
    pallas_call x1, Pallas kernels, widen(): pl.pallas_call(widen_kernel, grid=(8,), out_shape=(jax.ShapeDtypeStruct((...  11.1 us

profile of v3, /device:TPU:0, one launch (start us, length us, event | category | flops | bytes accessed | tf_op | source)
XLA Modules:
  0.0 184.9 jit_solution(13217638136849745495)
XLA Ops:
  0.7 32.6 %shard_map.297 = (bf16[512,2304]{1,0:T(8,128)(2,1)}, bf16[512,768]{1,0:T(8,128)(2,1)}, bf16[512,2304]{1,0:T(8,128)(2,1)}, bf16[512,768]{1,0:T(8,128)(2,1)}, f32[...) custom-call(bf16[512,768]{1,0:T(8,128)(2,1)} %bitcast.7, ...), custom_call_target="tpu_custom_call" | custom-call | tf_op jit(solution)/shard_map/pallas_call | solution.py:305
  33.2 137.5 %shard_map.298 = (bf16[24,2,2,96,384]{4,3,2,1,0:T(8,128)(2,1)}, bf16[512,768]{1,0:T(8,128)(2,1)}, bf16[512,768]{1,0:T(8,128)(2,1)}, f32[16,384]{1,0:T(8,128)}) custom-call(bf16[512,768]{1,0:T(8,128)(2,1)} %bitcast.9, bf16[768,768]{1,0:T(8,128)(2,1)} %wo_h.1, bf16[512,2304]{1,0:T(8,128)(2,1)} %get-tuple-element.34.qkv_h, ...), custom_call_target="tpu_custom_call" | custom-call | tf_op jit(solution)/shard_map/pallas_call | solution.py:806
  170.7 0.0 copy-start.2
  170.8 0.0 copy-start.1
  170.8 0.0 copy-start
  170.8 11.1 %shard_map.299 = (f32[1536,768]{1,0:T(8,128)}, f32[384,3072]{1,0:T(8,128)}, f32[384,768]{1,0:T(8,128)}, f32[384,2304]{1,0:T(8,128)}) custom-call(bf16[24,384,384]{2,1,0:T(8,128)(2,1)} %bitcast.5, bf16[24,384,384]{2,1,0:T(8,128)(2,1)} %bitcast.6), custom_call_target="tpu_custom_call" | custom-call | tf_op jit(solution)/shard_map/pallas_call | solution.py:888
  181.9 0.0 copy-done.2
  181.9 0.6 slice_reduce_fusion
  182.6 0.6 reshape.39
  183.2 0.0 copy-done.1
  183.2 0.9 copy.36
  184.0 0.0 copy-done
  184.0 0.9 copy.37
  (1 shorter events, 0.0 us)
Async XLA Ops:
  170.7 11.2 %copy-start.2 = (f32[16,384]{1,0:T(8,128)S(1)}, f32[16,384]{1,0:T(8,128)}, u32[]{:S(2)}) copy-start(f32[16,384]{1,0:T(8,128)} %get-tuple-element.46) | copy-start | bytes 73732
  170.8 12.4 %copy-start.1 = (bf16[512,768]{1,0:T(8,128)(2,1)S(1)}, bf16[512,768]{1,0:T(8,128)(2,1)}, u32[]{:S(2)}) copy-start(bf16[512,768]{1,0:T(8,128)(2,1)} %get-tuple-element.44) | copy-start | bytes 2359300
  170.8 13.3 %copy-start = (bf16[512,768]{1,0:T(8,128)(2,1)S(1)}, bf16[512,768]{1,0:T(8,128)(2,1)}, u32[]{:S(2)}) copy-start(bf16[512,768]{1,0:T(8,128)(2,1)} %get-tuple-element.45) | copy-start | bytes 2359300

commit v4 on v3

--- a/solution.py
+++ b/solution.py
@@ -361,9 +361,9 @@
 T_FORWARD = (0, 0, 1, 2, 3, 4, 5, 6)
 EMIT_DOWN, EMIT_UP, EMIT_OUT, EMIT_QKV = (0, 2, 4, 6), (8, 10, 12, 14), (16,), (18, 19, 20, 21, 22, 23)
 T_SECOND, T_ATTENDED = (7,), (8,)
-T_SEND = (8, 9, 9, 10, 11, 11, 12, 13, 13, 14, 15, 15)
-T_OWN = (8, 9, 10, 13, 14, 15)
-T_FAR = (12, 13, 14, 16, 17, 18)
+T_SEND = (8, 9, 10, 11, 12, 13, 14, 15, 16, 17, 18, 19)
+T_OWN = (8, 9, 10, 12, 14, 16)
+T_FAR = (11, 13, 15, 17, 19, 21)
 T_OUTPUT = (19, 19, 20, 20, 21, 21, 22, 22)
 T_GRAD = (24, 24, 25)
 T_FIRST = (26,)

time: 185 us -> 189 us (1.022)
  Pallas kernels: 181 us -> 185 us
    pallas_call x1, Pallas kernels: 138 us -> 141 us  [backward(): pl.pallas_call(halves_kernel, out_shape=(jax.ShapeDtypeStruct((CHUNKS, 2,...]
where the time goes in v4:
time: 189 us
  Pallas kernels  185 us (98%)
  local copies, waits for them, and re-layouts  3.02 us (2%)
    pallas_call x1, Pallas kernels, backward(): pl.pallas_call(halves_kernel, out_shape=(jax.ShapeDtypeStruct((CHUNKS, 2,...  141 us
    pallas_call x1, Pallas kernels, first_half(): pl.pallas_call(first_kernel, out_shape=tuple((jax.ShapeDtypeStruct((HALF,...  32.6 us
    pallas_call x1, Pallas kernels, widen(): pl.pallas_call(widen_kernel, grid=(8,), out_shape=(jax.ShapeDtypeStruct((...  11.1 us

profile of v4, /device:TPU:0, one launch (start us, length us, event | category | flops | bytes accessed | tf_op | source)
XLA Modules:
  0.0 188.7 jit_solution(7997153272277148416)
XLA Ops:
  0.7 32.6 %shard_map.297 = (bf16[512,2304]{1,0:T(8,128)(2,1)}, bf16[512,768]{1,0:T(8,128)(2,1)}, bf16[512,2304]{1,0:T(8,128)(2,1)}, bf16[512,768]{1,0:T(8,128)(2,1)}, f32[...) custom-call(bf16[512,768]{1,0:T(8,128)(2,1)} %bitcast.7, ...), custom_call_target="tpu_custom_call" | custom-call | tf_op jit(solution)/shard_map/pallas_call | solution.py:305
  33.2 141.3 %shard_map.298 = (bf16[24,2,2,96,384]{4,3,2,1,0:T(8,128)(2,1)}, bf16[512,768]{1,0:T(8,128)(2,1)}, bf16[512,768]{1,0:T(8,128)(2,1)}, f32[16,384]{1,0:T(8,128)}) custom-call(bf16[512,768]{1,0:T(8,128)(2,1)} %bitcast.9, bf16[768,768]{1,0:T(8,128)(2,1)} %wo_h.1, bf16[512,2304]{1,0:T(8,128)(2,1)} %get-tuple-element.34.qkv_h, ...), custom_call_target="tpu_custom_call" | custom-call | tf_op jit(solution)/shard_map/pallas_call | solution.py:806
  174.6 0.0 copy-start.2
  174.6 0.0 copy-start.1
  174.6 0.0 copy-start
  174.6 11.1 %shard_map.299 = (f32[1536,768]{1,0:T(8,128)}, f32[384,3072]{1,0:T(8,128)}, f32[384,768]{1,0:T(8,128)}, f32[384,2304]{1,0:T(8,128)}) custom-call(bf16[24,384,384]{2,1,0:T(8,128)(2,1)} %bitcast.5, bf16[24,384,384]{2,1,0:T(8,128)(2,1)} %bitcast.6), custom_call_target="tpu_custom_call" | custom-call | tf_op jit(solution)/shard_map/pallas_call | solution.py:888
  185.7 0.0 copy-done.2
  185.7 0.6 slice_reduce_fusion
  186.4 0.6 reshape.39
  187.0 0.0 copy-done.1
  187.0 0.9 copy.36
  187.9 0.0 copy-done
  187.9 0.9 copy.37
  (1 shorter events, 0.0 us)
Async XLA Ops:
  174.6 11.2 %copy-start.2 = (f32[16,384]{1,0:T(8,128)S(1)}, f32[16,384]{1,0:T(8,128)}, u32[]{:S(2)}) copy-start(f32[16,384]{1,0:T(8,128)} %get-tuple-element.46) | copy-start | bytes 73732
  174.6 12.4 %copy-start.1 = (bf16[512,768]{1,0:T(8,128)(2,1)S(1)}, bf16[512,768]{1,0:T(8,128)(2,1)}, u32[]{:S(2)}) copy-start(bf16[512,768]{1,0:T(8,128)(2,1)} %get-tuple-element.44) | copy-start | bytes 2359300
  174.6 13.3 %copy-start = (bf16[512,768]{1,0:T(8,128)(2,1)S(1)}, bf16[512,768]{1,0:T(8,128)(2,1)}, u32[]{:S(2)}) copy-start(bf16[512,768]{1,0:T(8,128)(2,1)} %get-tuple-element.45) | copy-start | bytes 2359300
